TPU v7x, 32 devices: a whole 2x2x4 slice. The times are simulated.
32 devices in a mesh: seq: 8 (over z, x), head: 4 (over y, core).
Axes of the slice: x: 2, y: 2, z: 4, core: 2. Of those that a mesh axis runs over, the one named last changes fastest.
Arguments:
- query_rows: bfloat16 [16384, 1024], P('seq', 'head'), may hold values from -8 to 8
- key_rows: bfloat16 [16384, 1024], P('seq', 'head'), may hold values from -6 to 6
- value_rows: bfloat16 [16384, 1024], P('seq', 'head'), may hold values from -12 to 12
- out_grad: bfloat16 [16384, 1024], P('seq', 'head'), may hold values from -12 to 12
- block_perm: int32 [8, 64], P('head'), may hold values from 0 to 63, as said below
- cut_count: int32 [8], P('head'), may hold values from 1 to 4, as said below
- norm_gain: float32 [1024], P('head'), may hold values from 0.1 to 1.9
Outputs:
- normed_out: bfloat16 [16384, 1024], P('seq', 'head')
- query_grad: bfloat16 [16384, 1024], P('seq', 'head')
- key_grad: bfloat16 [16384, 1024], P('seq', 'head')
- value_grad: bfloat16 [16384, 1024], P('seq', 'head')
- gain_grad: float32 [1024], P('head')
Inputs may be any that keep to these rules, and one draw needn't show every extreme that they name: `block_perm`: each row is a permutation of 0 to 63. For every head, of the 8 blocks d * 8 to (d + 1) * 8 - 1, at most 1 are paired with blocks of one range s * 8 to (s + 1) * 8 - 1, and some pair (d, s) reaches 1. `cut_count`: some head has exactly 4.
All inputs are finite; a program needn't handle non-finite values.
Results may differ from a plain program's by a relative error of at most 0.0071.
Values may be sent and summed in bfloat16 or wider, within the bound.
A program may use at most 128 MiB of HBM per device.

v0:
```python
from functools import partial

import jax
import jax.numpy as jnp
from jax import lax
from jax.sharding import PartitionSpec as P

BLOCK = 256
KCUT = 4


def split_heads(rows, heads):
    tokens = rows.shape[0]
    width = rows.shape[1] // heads
    return rows.reshape(tokens // BLOCK, BLOCK, heads, width).transpose(2, 0, 1, 3)


def merge_heads(parts):
    return parts.transpose(1, 2, 0, 3).reshape(
        parts.shape[1] * parts.shape[2], parts.shape[0] * parts.shape[3]
    )


def to_slots(rows, slot_of, count):
    match = slot_of[:, None, :] == jnp.arange(count)[None, :, None]
    chosen = jnp.sum(jnp.where(match, jnp.arange(rows.shape[1])[None, None, :], 0), axis=2)
    filled = jnp.any(match, axis=2)
    picked = jax.vmap(lambda piece, which: piece[which])(rows, chosen)
    shape = filled.shape + (1,) * (rows.ndim - 2)
    return jnp.where(filled.reshape(shape), picked, jnp.zeros_like(picked))


def from_slots(slot_rows, slot_of):
    return jax.vmap(lambda piece, which: piece[which])(slot_rows, slot_of)


def attend(query, own_rows, paired_rows, cutoff_rows, live, scale):
    width = query.shape[-1]
    span = own_rows.shape[1]
    count = cutoff_rows.shape[0]
    own = jnp.einsum(
        "gqd,gkd->gqk", query, own_rows[..., :width], preferred_element_type=jnp.float32
    )
    pair = jnp.einsum(
        "gqd,gkd->gqk", query, paired_rows[..., :width], preferred_element_type=jnp.float32
    )
    cut = jnp.einsum(
        "gqd,ckd->gqck", query, cutoff_rows[..., :width], preferred_element_type=jnp.float32
    )
    cut = cut.reshape(query.shape[0], query.shape[1], count * span)
    scores = jnp.concatenate([own, pair, cut], axis=-1) * scale
    open_keys = jnp.concatenate([jnp.ones((2 * span,), jnp.bool_), jnp.repeat(live, span)])
    scores = jnp.where(open_keys, scores, -1e30)
    top = jnp.max(scores, axis=-1)
    weights = jnp.exp(scores - top[..., None])
    total = jnp.sum(weights, axis=-1)
    return (weights / total[..., None], top, total)


def forward_head(query, own_rows, paired_rows, cutoff_rows, live, scale):
    width = query.shape[-1]
    span = query.shape[1]
    groups = query.shape[0] // 2
    count = cutoff_rows.shape[0]

    def forward_step(pieces):
        query_part, own_part, pair_part = pieces
        prob, top, total = attend(query_part, own_part, pair_part, cutoff_rows, live, scale)
        weights = prob.astype(jnp.bfloat16)
        result = jnp.einsum(
            "gqk,gkd->gqd",
            weights[..., :span],
            own_part[..., width:],
            preferred_element_type=jnp.float32,
        )
        result = result + jnp.einsum(
            "gqk,gkd->gqd",
            weights[..., span : 2 * span],
            pair_part[..., width:],
            preferred_element_type=jnp.float32,
        )
        cut_weight = weights[..., 2 * span :].reshape(2, span, count, span)
        result = result + jnp.einsum(
            "gqck,ckd->gqd",
            cut_weight,
            cutoff_rows[..., width:],
            preferred_element_type=jnp.float32,
        )
        return result.astype(jnp.bfloat16)

    result = lax.map(
        forward_step,
        (
            query.reshape(groups, 2, span, width),
            own_rows.reshape(groups, 2, span, 2 * width),
            paired_rows.reshape(groups, 2, span, 2 * width),
        ),
    )
    return result.reshape(query.shape)


def backward_head(query, own_rows, paired_rows, cutoff_rows, live, cotangent, scale):
    width = query.shape[-1]
    span = query.shape[1]
    groups = query.shape[0] // 2
    count = cutoff_rows.shape[0]

    def backward_step(carry, pieces):
        query_part, own_part, pair_part, cot_part = pieces
        prob, top, total = attend(query_part, own_part, pair_part, cutoff_rows, live, scale)
        weights = prob.astype(jnp.bfloat16)
        dprob = jnp.concatenate(
            [
                jnp.einsum(
                    "gqd,gkd->gqk",
                    cot_part,
                    own_part[..., width:],
                    preferred_element_type=jnp.float32,
                ),
                jnp.einsum(
                    "gqd,gkd->gqk",
                    cot_part,
                    pair_part[..., width:],
                    preferred_element_type=jnp.float32,
                ),
                jnp.einsum(
                    "gqd,ckd->gqck",
                    cot_part,
                    cutoff_rows[..., width:],
                    preferred_element_type=jnp.float32,
                ).reshape(2, span, count * span),
            ],
            axis=-1,
        )
        delta = jnp.sum(prob * dprob, axis=-1)
        dscore = (prob * (dprob - delta[..., None]) * scale).astype(jnp.bfloat16)
        cut_score = dscore[..., 2 * span :].reshape(2, span, count, span)
        cut_weight = weights[..., 2 * span :].reshape(2, span, count, span)
        query_grad = jnp.einsum(
            "gqk,gkd->gqd",
            dscore[..., :span],
            own_part[..., :width],
            preferred_element_type=jnp.float32,
        )
        query_grad = query_grad + jnp.einsum(
            "gqk,gkd->gqd",
            dscore[..., span : 2 * span],
            pair_part[..., :width],
            preferred_element_type=jnp.float32,
        )
        query_grad = query_grad + jnp.einsum(
            "gqck,ckd->gqd", cut_score, cutoff_rows[..., :width], preferred_element_type=jnp.float32
        )
        own_grad = jnp.concatenate(
            [
                jnp.einsum(
                    "gqk,gqd->gkd",
                    dscore[..., :span],
                    query_part,
                    preferred_element_type=jnp.float32,
                ),
                jnp.einsum(
                    "gqk,gqd->gkd",
                    weights[..., :span],
                    cot_part,
                    preferred_element_type=jnp.float32,
                ),
            ],
            axis=-1,
        )
        pair_grad = jnp.concatenate(
            [
                jnp.einsum(
                    "gqk,gqd->gkd",
                    dscore[..., span : 2 * span],
                    query_part,
                    preferred_element_type=jnp.float32,
                ),
                jnp.einsum(
                    "gqk,gqd->gkd",
                    weights[..., span : 2 * span],
                    cot_part,
                    preferred_element_type=jnp.float32,
                ),
            ],
            axis=-1,
        )
        cut_grad = jnp.concatenate(
            [
                jnp.einsum(
                    "gqck,gqd->ckd", cut_score, query_part, preferred_element_type=jnp.float32
                ),
                jnp.einsum(
                    "gqck,gqd->ckd", cut_weight, cot_part, preferred_element_type=jnp.float32
                ),
            ],
            axis=-1,
        )
        return (
            carry + cut_grad,
            (query_grad.astype(jnp.bfloat16), own_grad, pair_grad, top, total, delta),
        )

    start = jnp.zeros((count, span, 2 * width), jnp.float32)
    cut_sum, outputs = lax.scan(
        backward_step,
        start,
        (
            query.reshape(groups, 2, span, width),
            own_rows.reshape(groups, 2, span, 2 * width),
            paired_rows.reshape(groups, 2, span, 2 * width),
            cotangent.reshape(groups, 2, span, width),
        ),
    )
    query_grad, own_grad, pair_grad, top, total, delta = outputs
    blocks = query.shape[0]
    return (
        query_grad.reshape(query.shape),
        own_grad.reshape(own_rows.shape),
        pair_grad.reshape(own_rows.shape),
        cut_sum,
        top.reshape(blocks, span),
        total.reshape(blocks, span),
        delta.reshape(blocks, span),
    )


def owner_pair(query, cotangent, top, total, delta, own_rows, scale):
    width = query.shape[-1]
    scores = (
        jnp.einsum("jqd,jkd->jqk", query, own_rows[..., :width], preferred_element_type=jnp.float32)
        * scale
    )
    prob = jnp.exp(scores - top[..., None]) / total[..., None]
    dprob = jnp.einsum(
        "jqd,jkd->jqk", cotangent, own_rows[..., width:], preferred_element_type=jnp.float32
    )
    dscore = (prob * (dprob - delta[..., None]) * scale).astype(jnp.bfloat16)
    return jnp.concatenate(
        [
            jnp.einsum("jqk,jqd->jkd", dscore, query, preferred_element_type=jnp.float32),
            jnp.einsum(
                "jqk,jqd->jkd",
                prob.astype(jnp.bfloat16),
                cotangent,
                preferred_element_type=jnp.float32,
            ),
        ],
        axis=-1,
    )


def body(query_rows, key_rows, value_rows, out_grad, block_perm, cut_count, norm_gain):
    heads = block_perm.shape[0]
    width = query_rows.shape[1] // heads
    blocks = query_rows.shape[0] // BLOCK
    seq_count = lax.axis_size("seq")
    head_count = lax.axis_size("head")
    capacity = (blocks + seq_count - 1) // seq_count
    slot_count = seq_count * capacity
    scale = width ** (-0.5)
    position = lax.axis_index("seq")
    query_h = split_heads(query_rows, heads)
    grad_h = split_heads(out_grad, heads)
    own_rows = jnp.concatenate(
        [split_heads(key_rows, heads), split_heads(value_rows, heads)], axis=-1
    )
    local_perm = lax.dynamic_slice_in_dim(block_perm, position * blocks, blocks, 1)
    source_dev = local_perm // blocks
    lower = jnp.arange(blocks)[:, None] > jnp.arange(blocks)[None, :]
    same_source = source_dev[:, :, None] == source_dev[:, None, :]
    recv_slot = source_dev * capacity + jnp.sum(same_source & lower[None], axis=2)
    owned = position * blocks + jnp.arange(blocks)
    hits = block_perm[:, None, :] == owned[None, :, None]
    dest_global = jnp.sum(
        jnp.where(hits, jnp.arange(block_perm.shape[1])[None, None, :], 0), axis=2
    )
    dest_dev = dest_global // blocks
    dest_local = dest_global % blocks
    before = (dest_dev[:, :, None] == dest_dev[:, None, :]) & (
        dest_local[:, None, :] < dest_local[:, :, None]
    )
    send_slot = dest_dev * capacity + jnp.sum(before, axis=2)
    own_send = to_slots(own_rows, send_slot, slot_count)
    query_send = to_slots(query_h, recv_slot, slot_count)
    own_recv, query_recv = (
        lax.all_to_all(own_send, "seq", split_axis=1, concat_axis=1, tiled=True),
        lax.all_to_all(query_send, "seq", split_axis=1, concat_axis=1, tiled=True),
    )
    query_owner = from_slots(query_recv, send_slot)
    paired_rows = from_slots(own_recv, recv_slot)
    cut_global = block_perm[:, :KCUT]
    cut_dev = cut_global // blocks
    cut_local = cut_global % blocks
    cut_pick = jax.vmap(lambda piece, which: piece[which])(own_rows, cut_local)
    cut_pick = jnp.where(
        (cut_dev == position)[:, :, None, None], cut_pick, jnp.zeros_like(cut_pick)
    )
    cutoff_rows = lax.psum(cut_pick.astype(jnp.float32).astype(jnp.bfloat16), "seq")
    live = jnp.arange(KCUT)[None, :] < cut_count[:, None]
    attn = jax.vmap(partial(forward_head, scale=scale))(
        query_h, own_rows, paired_rows, cutoff_rows, live
    )
    attn_f = attn.astype(jnp.float32)
    grad_f = grad_h.astype(jnp.float32)
    gain = norm_gain.reshape(heads, 1, 1, width)
    square_part = jnp.sum(attn_f * attn_f, axis=(0, 3))
    mix_part = jnp.sum(gain * grad_f * attn_f, axis=(0, 3))
    square_sum, mix_sum = lax.psum((square_part, mix_part), "head")
    features = head_count * heads * width
    scale_row = lax.rsqrt(square_sum / features + 1e-06)[None, :, :, None]
    normed = (attn_f * scale_row * gain).astype(jnp.bfloat16)
    gain_part = jnp.sum(grad_f * attn_f * scale_row, axis=(1, 2))
    cotangent = (
        scale_row * gain * grad_f - attn_f * scale_row**3 * mix_sum[None, :, :, None] / features
    ).astype(jnp.bfloat16)
    query_grad, own_grad, pair_grad, cut_grad, top, total, delta = jax.vmap(
        partial(backward_head, scale=scale)
    )(query_h, own_rows, paired_rows, cutoff_rows, live, cotangent)
    cot_send = to_slots(cotangent, recv_slot, slot_count)
    cot_recv = lax.all_to_all(cot_send, "seq", split_axis=1, concat_axis=1, tiled=True)
    top_send = to_slots(top, recv_slot, slot_count)
    total_send = to_slots(total, recv_slot, slot_count)
    delta_send = to_slots(delta, recv_slot, slot_count)
    top_recv, total_recv, delta_recv = (
        lax.all_to_all(top_send, "seq", split_axis=1, concat_axis=1, tiled=True),
        lax.all_to_all(total_send, "seq", split_axis=1, concat_axis=1, tiled=True),
        lax.all_to_all(delta_send, "seq", split_axis=1, concat_axis=1, tiled=True),
    )
    pair_full = jax.vmap(partial(owner_pair, scale=scale))(
        query_owner,
        from_slots(cot_recv, send_slot),
        from_slots(top_recv, send_slot),
        from_slots(total_recv, send_slot),
        from_slots(delta_recv, send_slot),
        own_rows,
    )
    pair_term = lax.optimization_barrier(pair_full.astype(jnp.bfloat16)).astype(jnp.float32)
    cut_total, gain_total = lax.psum((cut_grad, gain_part), "seq")
    match = (
        (cut_dev == position)[:, :, None]
        & (cut_local[:, :, None] == jnp.arange(blocks)[None, None, :])
    ).astype(jnp.float32)
    cut_term = jnp.einsum("hcj,hcqd->hjqd", match, cut_total, precision=lax.Precision.HIGHEST)
    total_grad = (own_grad + pair_term + cut_term).astype(jnp.bfloat16)
    return (
        merge_heads(normed),
        merge_heads(query_grad),
        merge_heads(total_grad[..., :width]),
        merge_heads(total_grad[..., width:]),
        gain_total.reshape(heads * width),
    )


def solution(mesh):
    placed = (
        P("seq", "head"),
        P("seq", "head"),
        P("seq", "head"),
        P("seq", "head"),
        P("head", None),
        P("head"),
        P("head"),
    )
    return jax.shard_map(
        body,
        mesh=mesh,
        in_specs=placed,
        out_specs=(
            P("seq", "head"),
            P("seq", "head"),
            P("seq", "head"),
            P("seq", "head"),
            P("head"),
        ),
        check_vma=False,
    )
```

profile of v0, /device:TPU:0, one launch (start us, length us, event | category | flops | bytes accessed | tf_op | source)
XLA Modules:
  0.0 683.0 jit_solution(10543006544791201384)
XLA Ops:
  19.0 7.3 %all-to-all-start = ((bf16[2,8,256,256]{3,2,0,1:T(8,128)(2,1)}), bf16[2,8,256,256]{3,2,0,1:T(8,128)(2,1)}, u32[]{:S(2)}, u32[]{:S(2)}) async-start(bf16[2,8,256,256]{3,2,0,1:T(8,128)(2,1)} %copy_select_fusion), calls=%async_computation | async-start | bytes 4194304 | tf_op jit(solution)/shard_map/all_to_all | solution.py:287
  36.0 51.3 %all-to-all-done = bf16[2,8,256,256]{3,2,0,1:T(8,128)(2,1)} async-done(((bf16[2,8,256,256]{3,2,0,1:T(8,128)(2,1)}), bf16[2,8,256,256]{3,2,0,1:T(8,128)(2,1)}, u32[]{:S(2)}, u32[]{:S(2)}) %all-to-all-start) | async-done | bytes 2097184 | tf_op jit(solution)/shard_map/all_to_all | solution.py:287
  94.2 40.7 %all-reduce.5.cloned.1.call-done = bf16[2,4,256,256]{3,2,1,0:T(8,128)(2,1)} async-done(((bf16[2,4,256,256]{3,2,1,0:T(8,128)(2,1)}), bf16[2,4,256,256]{3,2,1,0:T(8,128)(2,1)}) %all-reduce.5.cloned.1.call-update) | async-done | bytes 1048592 | tf_op jit(solution)/shard_map/psum | solution.py:299
  136.1 76.6 %while.32 = (s32[]{:T(128)}, bf16[4,2,2,256,128]{4,3,2,0,1:T(8,128)(2,1)}, bf16[4,2,2,256,128]{4,3,2,1,0:T(8,128)(2,1)S(1)}, bf16[4,2,2,256,256]{4,3,2,1,0:T(8,1...) while((s32[]{:T(128)}, ...), condition=%wide.region_9.10_spmd.clone, body=%wide.region_6.9_spmd.clone.sunk | while | flops 818284032 | bytes 55597728 | solution.py:91
  142.7 5.4 copy.414
  161.8 5.4 copy.414
  181.0 5.4 copy.414
  200.1 5.4 copy.414
  217.2 6.9 %psum.36 = f32[8,256]{1,0:T(8,128)S(1)} all-reduce(f32[8,256]{1,0:T(8,128)S(1)} %reduce_sum.131), channel_id=1, replica_groups=mesh['seq'=8,'head'=4] {'head'}, use_global_device_ids=true, to_apply=%region_11.12 | all-reduce | flops 2048 | bytes 16384 | tf_op jit(solution)/shard_map/psum | solution.py:309
  227.0 6.3 psum.37
  237.7 237.2 %while.33 = (s32[]{:T(128)}, f32[2,4,256,256]{2,3,1,0:T(8,128)}, bf16[4,2,2,256,128]{4,3,2,0,1:T(8,128)(2,1)}, f32[4,2,2,256,256]{3,4,2,1,0:T(8,128)}, f32[4,2,2...) while((s32[]{:T(128)}, f32[2,4,256,256]{2,3,1,0:T(8,128)}, ...), condition=%wide.region_18.19_spmd.clone, body=%wide.region_14.18_spmd.clone.sunk | while | flops 1934750720 | bytes 244144336 | solution.py:205
  243.4 5.4 copy.417
  258.1 5.4 copy.416
  263.5 5.6 multiply_reduce_fusion.3
  316.8 5.4 copy.416
  322.2 5.6 multiply_reduce_fusion.3
  376.3 5.4 copy.416
  381.7 5.6 multiply_reduce_fusion.3
  435.8 5.4 copy.416
  441.2 5.6 multiply_reduce_fusion.3
  477.6 9.9 %all_to_all.30 = f32[2,8,256]{2,0,1:T(2,128)S(1)} all-to-all(f32[2,8,256]{2,0,1:T(2,128)S(1)} %get-tuple-element.372), channel_id=1, replica_groups=mesh['seq'=8,'head'=4] {'seq'}, dimensions={1} | all-to-all | bytes 32768 | tf_op jit(solution)/shard_map/all_to_all | solution.py:326
  508.2 26.6 %all_to_all.31 = bf16[2,8,256,128]{3,2,0,1:T(8,128)(2,1)} all-to-all(bf16[2,8,256,128]{3,2,0,1:T(8,128)(2,1)} %get-tuple-element.373), channel_id=1, replica_groups=mesh['seq'=8,'head'=4] {'seq'}, dimensions={1} | all-to-all | bytes 2097152 | tf_op jit(solution)/shard_map/all_to_all | solution.py:288
  549.6 28.1 %psum.39 = f32[256]{0:T(256)} all-reduce(f32[256]{0:T(256)S(1)} %bitcast.413), channel_id=1, replica_groups=mesh['seq'=8,'head'=4] {'seq'}, use_global_device_ids=true, to_apply=%region_23.24 | all-reduce | flops 256 | bytes 2048 | tf_op jit(solution)/shard_map/psum | solution.py:339
  593.5 63.7 %all-reduce.7.cloned.1.call-done = f32[2,4,256,256]{3,1,2,0:T(4,128)} async-done(((f32[2,4,256,256]{3,1,2,0:T(4,128)}), f32[2,4,256,256]{3,1,2,0:T(4,128)}) %all-reduce.7.cloned.1.call-update) | async-done | bytes 2097168 | tf_op jit(solution)/shard_map/psum | solution.py:339
  (478 shorter events, 355.4 us)
Async XLA Ops:
  15.9 10.5 %copy-start.31 = (s32[2,64]{1,0:T(2,128)S(1)}, s32[2,64]{1,0:T(2,128)}, u32[]{:S(2)}) copy-start(s32[2,64]{1,0:T(2,128)} %param.15) | copy-start | bytes 1540
  19.0 68.4 %all-to-all-start = ((bf16[2,8,256,256]{3,2,0,1:T(8,128)(2,1)}), bf16[2,8,256,256]{3,2,0,1:T(8,128)(2,1)}, u32[]{:S(2)}, u32[]{:S(2)}) async-start(bf16[2,8,256,256]{3,2,0,1:T(8,128)(2,1)} %copy_select_fusion), calls=%async_computation | async-start | bytes 4194304 | tf_op jit(solution)/shard_map/all_to_all | solution.py:287
  26.3 108.6 %all-reduce.5.cloned.1.call-start = ((), (), s32[]{:S(2)}) async-start(), calls=%async_computation.6 | async-start | bytes 2097152 | tf_op jit(solution)/shard_map/psum | solution.py:299
  89.1 47.0 %copy-start.42 = (s32[2]{0:T(128)S(1)}, s32[2]{0:T(128)}, u32[]{:S(2)}) copy-start(s32[2]{0:T(128)} %param.16) | copy-start | bytes 28
  212.7 11.5 %copy-start.19 = (f32[8,256,2,128]{3,2,1,0:T(2,128)S(1)}, f32[8,256,2,128]{3,2,1,0:T(2,128)}, u32[]{:S(2)}) copy-start(f32[8,256,2,128]{3,2,1,0:T(2,128)} %reshape.418) | copy-start | bytes 6291460
  212.7 11.5 %copy-start.41 = (f32[256]{0:T(256)S(1)}, f32[256]{0:T(256)}, u32[]{:S(2)}) copy-start(f32[256]{0:T(256)} %param.17) | copy-start | bytes 3076
  237.7 237.3 %copy-start.28 = (s32[16]{0:T(128)S(1)}, s32[16]{0:T(128)}, u32[]{:S(2)}) copy-start(s32[16]{0:T(128)} %reshape.321) | copy-start | bytes 196
  237.7 239.1 %copy-start.39 = (pred[2,8]{0,1:T(8,128)(4,1)S(1)}, pred[2,8]{0,1:T(8,128)(4,1)}, u32[]{:S(2)}) copy-start(pred[2,8]{0,1:T(8,128)(4,1)} %copy.288) | copy-start | bytes 52
  263.5 6.2 copy-start.2
  263.5 6.4 copy-start.6
  322.2 6.2 copy-start.2
  322.2 6.4 copy-start.6
  381.7 6.2 copy-start.2
  381.7 6.4 copy-start.6
  441.2 6.2 copy-start.2
  441.2 6.4 copy-start.6
  487.5 9.8 %all-to-all-start.3 = ((f32[2,8,256]{2,0,1:T(2,128)}), f32[2,8,256]{2,0,1:T(2,128)S(1)}, u32[]{:S(2)}, u32[]{:S(2)}) async-start(f32[2,8,256]{2,0,1:T(2,128)} %get-tuple-element.371), calls=%async_computation.3 | async-start | bytes 32768 | tf_op jit(solution)/shard_map/all_to_all | solution.py:327
  497.3 10.9 %all-to-all-start.5 = ((f32[2,8,256]{2,0,1:T(2,128)}), f32[2,8,256]{2,0,1:T(2,128)S(1)}, u32[]{:S(2)}, u32[]{:S(2)}) async-start(f32[2,8,256]{2,0,1:T(2,128)} %get-tuple-element.370), calls=%async_computation.5 | async-start | bytes 32768 | tf_op jit(solution)/shard_map/all_to_all | solution.py:328
  501.6 36.9 %copy-start.17 = (f32[2,4,256,256]{2,3,1,0:T(8,128)S(1)}, f32[2,4,256,256]{2,3,1,0:T(8,128)}, u32[]{:S(2)}) copy-start(f32[2,4,256,256]{2,3,1,0:T(8,128)} %get-tuple-element.120) | copy-start | bytes 6291460
  534.8 46.5 %all-to-all-start.4 = ((bf16[2,8,256,128]{3,2,0,1:T(8,128)(2,1)}), bf16[2,8,256,128]{3,2,0,1:T(8,128)(2,1)S(1)}, u32[]{:S(2)}, u32[]{:S(2)}) async-start(bf16[2,8,256,128]{3,2,0,1:T(8,128)(2,1)} %get-tuple-element.374), calls=%async_computation.4 | async-start | bytes 2097152 | tf_op jit(solution)/shard_map/all_to_all | solution.py:321
  538.5 118.7 %all-reduce.7.cloned.1.call-start = ((), (), s32[]{:S(2)}) async-start(), calls=%async_computation.7 | async-start | bytes 4194304 | tf_op jit(solution)/shard_map/psum | solution.py:339
  545.2 34.3 %copy-start.24 = (bf16[2,8,256,128]{3,2,0,1:T(8,128)(2,1)S(1)}, bf16[2,8,256,128]{3,2,0,1:T(8,128)(2,1)}, u32[]{:S(2)}) copy-start(bf16[2,8,256,128]{3,2,0,1:T(8,128)(2,1)} %all_to_all.31) | copy-start | bytes 3145732
  592.1 65.1 %copy-start.32 = (s32[2,4]{1,0:T(2,128)S(1)}, s32[2,4]{1,0:T(2,128)}, u32[]{:S(2)}) copy-start(s32[2,4]{1,0:T(2,128)} %get-tuple-element.351) | copy-start | bytes 100
  592.1 65.1 %copy-start.38 = (pred[2,4]{1,0:T(4,128)(4,1)S(1)}, pred[2,4]{1,0:T(4,128)(4,1)}, u32[]{:S(2)}) copy-start(pred[2,4]{1,0:T(4,128)(4,1)} %copy-done.37) | copy-start | bytes 28
  (79 other events, 254.6 us)
Sparse Core Ops, SparseCore 0:
  31.2 103.6 all-reduce.4
  542.9 114.2 all-reduce.6
where the time goes:
time: 686 us; the launch traced here: 683 us
  local copies, waits for them, and re-layouts  173 us (25%)
  waiting for transfers between devices  161 us (23%)
  matrix products  123 us (18%)
  other arithmetic  114 us (17%)
  blocking collectives  77.8 us (11%)
  starting transfers between devices  18.7 us (3%)
  between operations  14.6 us (2%)
    psum x1, waiting for transfers between devices, body(): cut_total, gain_total = lax.psum((cut_grad, gain_part), 'seq')  63.7 us
    all_to_all x1, waiting for transfers between devices, body(): lax.all_to_all(own_send, 'seq', split_axis=1, concat_axis=1, tiled=True)  51.3 us
    reshape x8, local copies, waits for them, and re-layouts, attend(): cut = cut.reshape(query.shape[0], query.shape[1], count * span)  43.2 us
    psum x1, waiting for transfers between devices, body(): lax.psum(cut_pick.astype(jnp.float32).astype(jnp.bfloat16), 'seq')  40.7 us
    psum x1, blocking collectives, body(): cut_total, gain_total = lax.psum((cut_grad, gain_part), 'seq')  28.1 us
    all_to_all x1, blocking collectives, body(): lax.all_to_all(query_send, 'seq', split_axis=1, concat_axis=1, tiled=True)  26.6 us
    reduce_sum x4, other arithmetic, backward_step(): delta = jnp.sum(prob * dprob, axis=-1)  22.4 us
    reshape x4, local copies, waits for them, and re-layouts, backward_step(): dprob = jnp.concatenate([jnp.einsum('gqd,gkd->gqk', cot_part, own_part[.....  21.7 us
  transfers between devices with their start and end apart: 6, of which 5 were waited for; matrix products, arithmetic and copies ran while one was open for 7% of the time, Pallas kernels for 0%

commit v1 on v0

v1 whole, which is shorter than its diff:
```python
import math

import jax
import jax.numpy as jnp
from jax import lax
from jax.experimental import pallas as pl
from jax.experimental.pallas import tpu as pltpu
from jax.sharding import PartitionSpec as P

BLOCK = 256
KCUT = 4
F32 = jnp.float32
BF16 = jnp.bfloat16
NT = (((1,), (1,)), ((), ()))
TN = (((0,), (0,)), ((), ()))
NN = (((1,), (0,)), ((), ()))
VMEM_LIMIT = 48 * 1024 * 1024


def dot(a, b, dims):
    return lax.dot_general(a, b, dims, preferred_element_type=F32)


def params(semantics):
    return pltpu.CompilerParams(
        dimension_semantics=semantics, vmem_limit_bytes=VMEM_LIMIT
    )


def cost(flops, nbytes):
    return pl.CostEstimate(flops=int(flops), bytes_accessed=int(nbytes), transcendentals=0)


def pack_kernel(kv_idx, q_idx, k_ref, v_ref, q_ref, kv_out, q_out):
    width = k_ref.shape[1]
    kv_out[0, 0, :, :width] = k_ref[...]
    kv_out[0, 0, :, width:] = v_ref[...]
    q_out[0, 0] = q_ref[...]


def pack(kv_idx, q_idx, keys, values, query, slots, heads, width):
    spec = pl.BlockSpec((BLOCK, width), lambda s, h, ki, qi: (ki[h, s], h))
    return pl.pallas_call(
        pack_kernel,
        grid_spec=pltpu.PrefetchScalarGridSpec(
            num_scalar_prefetch=2,
            grid=(slots, heads),
            in_specs=[
                spec,
                spec,
                pl.BlockSpec((BLOCK, width), lambda s, h, ki, qi: (qi[h, s], h)),
            ],
            out_specs=[
                pl.BlockSpec((1, 1, BLOCK, 2 * width), lambda s, h, ki, qi: (s, h, 0, 0)),
                pl.BlockSpec((1, 1, BLOCK, width), lambda s, h, ki, qi: (s, h, 0, 0)),
            ],
        ),
        out_shape=[
            jax.ShapeDtypeStruct((slots, heads, BLOCK, 2 * width), BF16),
            jax.ShapeDtypeStruct((slots, heads, BLOCK, width), BF16),
        ],
        compiler_params=params(("arbitrary", "arbitrary")),
        name="pack",
    )(kv_idx, q_idx, keys, values, query)


def cut_kernel(idx, mine, k_ref, v_ref, out):
    width = k_ref.shape[1]
    keep = mine[pl.program_id(0), pl.program_id(1)] > 0
    out[0, 0, :, :width] = jnp.where(keep, k_ref[...], jnp.zeros_like(k_ref))
    out[0, 0, :, width:] = jnp.where(keep, v_ref[...], jnp.zeros_like(v_ref))


def cut_pick(idx, mine, keys, values, heads, width):
    spec = pl.BlockSpec((BLOCK, width), lambda h, c, ci, mi: (ci[h, c], h))
    return pl.pallas_call(
        cut_kernel,
        grid_spec=pltpu.PrefetchScalarGridSpec(
            num_scalar_prefetch=2,
            grid=(heads, KCUT),
            in_specs=[spec, spec],
            out_specs=pl.BlockSpec((1, 1, BLOCK, 2 * width), lambda h, c, ci, mi: (h, c, 0, 0)),
        ),
        out_shape=jax.ShapeDtypeStruct((heads, KCUT, BLOCK, 2 * width), BF16),
        compiler_params=params(("arbitrary", "arbitrary")),
        name="cut_pick",
    )(idx, mine, keys, values)


def forward_kernel(
    slot, count, q_ref, k_ref, v_ref, pair_ref, cut_ref, g_ref, gain_ref, attn_out, stat_out, s_buf
):
    head = pl.program_id(0)
    width = q_ref.shape[1]
    factor = width ** (-0.5) * math.log2(math.e)

    def run(opened):
        query = q_ref[...]
        key_list = [k_ref[...], pair_ref[0, 0, :, :width]]
        value_list = [v_ref[...], pair_ref[0, 0, :, width:]]
        for c in range(opened):
            key_list.append(cut_ref[0, c, :, :width])
            value_list.append(cut_ref[0, c, :, width:])
        top = None
        for j, piece in enumerate(key_list):
            s = dot(piece, query, NT)
            s_buf[j] = s
            high = jnp.max(s, axis=0, keepdims=True)
            top = high if top is None else jnp.maximum(top, high)
        top = top * factor
        total = jnp.zeros_like(top)
        acc = jnp.zeros((width, BLOCK), F32)
        for j, piece in enumerate(value_list):
            e = jnp.exp2(s_buf[j] * factor - top)
            total = total + jnp.sum(e, axis=0, keepdims=True)
            acc = acc + dot(piece, e.astype(BF16), TN)
        attn_t = (acc / total).astype(BF16).astype(F32)
        attn_out[...] = attn_t.T.astype(BF16)
        grad_t = (g_ref[...].astype(F32) * gain_ref[...]).T
        lse = top + jnp.log2(total)
        square = jnp.sum(attn_t * attn_t, axis=0, keepdims=True)
        mix = jnp.sum(grad_t * attn_t, axis=0, keepdims=True)
        stat_out[0, 0] = jnp.concatenate(
            [lse, square, mix, jnp.zeros((5, BLOCK), F32)], axis=0
        )

    for opened in range(1, KCUT + 1):
        pl.when(count[head] == opened)(lambda opened=opened: run(opened))


def forward(slot, count, query, keys, values, pair, cut, grad, gain, heads, width, blocks):
    rows = pl.BlockSpec((BLOCK, width), lambda h, b, s, n: (b, h))
    return pl.pallas_call(
        forward_kernel,
        grid_spec=pltpu.PrefetchScalarGridSpec(
            num_scalar_prefetch=2,
            grid=(heads, blocks),
            in_specs=[
                rows,
                rows,
                rows,
                pl.BlockSpec((1, 1, BLOCK, 2 * width), lambda h, b, s, n: (s[h, b], h, 0, 0)),
                pl.BlockSpec((1, KCUT, BLOCK, 2 * width), lambda h, b, s, n: (h, 0, 0, 0)),
                rows,
                pl.BlockSpec((1, width), lambda h, b, s, n: (0, h)),
            ],
            out_specs=[
                rows,
                pl.BlockSpec((1, 1, 8, BLOCK), lambda h, b, s, n: (h, b, 0, 0)),
            ],
            scratch_shapes=[pltpu.VMEM((2 + KCUT, BLOCK, BLOCK), F32)],
        ),
        out_shape=[
            jax.ShapeDtypeStruct((blocks * BLOCK, heads * width), BF16),
            jax.ShapeDtypeStruct((heads, blocks, 8, BLOCK), F32),
        ],
        compiler_params=params(("arbitrary", "arbitrary")),
        cost_estimate=cost(
            4 * heads * blocks * BLOCK * BLOCK * 6 * width, 10 * blocks * BLOCK * heads * width
        ),
        name="forward",
    )(slot, count, query, keys, values, pair, cut, grad, gain)


def norm_kernel(
    slot, attn_ref, g_ref, gain_ref, stat_ref, row_ref, norm_out, cot_out, send_out, gain_out
):
    width = attn_ref.shape[1]
    attn = attn_ref[...].astype(F32)
    grad = g_ref[...].astype(F32)
    gain = gain_ref[...]
    scale = jnp.broadcast_to(row_ref[0, 0:1, :], (width, BLOCK)).T
    coef = jnp.broadcast_to(row_ref[0, 1:2, :], (width, BLOCK)).T
    scaled = attn * scale
    norm_out[...] = (scaled * gain).astype(BF16)
    cot = (scale * gain * grad - attn * coef).astype(BF16)
    cot_out[0, 0] = cot
    delta = jnp.sum((cot.astype(F32) * attn).T, axis=0, keepdims=True)
    send_out[0, 0] = jnp.concatenate(
        [stat_ref[0, 0, 0:1, :], delta, jnp.zeros((6, BLOCK), F32)], axis=0
    )
    part = jnp.sum((grad * scaled).reshape(BLOCK // 8, 8, width), axis=0)

    @pl.when(pl.program_id(1) == 0)
    def _():
        gain_out[0] = part

    @pl.when(pl.program_id(1) > 0)
    def _():
        gain_out[0] = gain_out[0] + part


def norm(slot, attn, grad, gain, stat, row, heads, width, blocks, slots):
    rows = pl.BlockSpec((BLOCK, width), lambda h, b, s: (b, h))
    return pl.pallas_call(
        norm_kernel,
        grid_spec=pltpu.PrefetchScalarGridSpec(
            num_scalar_prefetch=1,
            grid=(heads, blocks),
            in_specs=[
                rows,
                rows,
                pl.BlockSpec((1, width), lambda h, b, s: (0, h)),
                pl.BlockSpec((1, 1, 8, BLOCK), lambda h, b, s: (h, b, 0, 0)),
                pl.BlockSpec((1, 2, BLOCK), lambda h, b, s: (b, 0, 0)),
            ],
            out_specs=[
                rows,
                pl.BlockSpec((1, 1, BLOCK, width), lambda h, b, s: (s[h, b], h, 0, 0)),
                pl.BlockSpec((1, 1, 8, BLOCK), lambda h, b, s: (s[h, b], h, 0, 0)),
                pl.BlockSpec((1, 8, width), lambda h, b, s: (h, 0, 0)),
            ],
        ),
        out_shape=[
            jax.ShapeDtypeStruct((blocks * BLOCK, heads * width), BF16),
            jax.ShapeDtypeStruct((slots, heads, BLOCK, width), BF16),
            jax.ShapeDtypeStruct((slots, heads, 8, BLOCK), F32),
            jax.ShapeDtypeStruct((heads, 8, width), F32),
        ],
        compiler_params=params(("arbitrary", "arbitrary")),
        name="norm",
    )(slot, attn, grad, gain, stat, row)


def backward_kernel(
    slot, count, q_ref, k_ref, v_ref, pair_ref, cut_ref, cot_ref, stat_ref, dq_out, own_out, cut_out
):
    head = pl.program_id(0)
    width = q_ref.shape[1]
    scale = width ** (-0.5)
    factor = scale * math.log2(math.e)

    @pl.when(pl.program_id(1) == 0)
    def _():
        cut_out[...] = jnp.zeros_like(cut_out)

    def run(opened):
        query = q_ref[...]
        cot = cot_ref[0, 0]
        lse = stat_ref[0, 0, 0:1, :]
        delta = stat_ref[0, 0, 1:2, :]
        key_list = [k_ref[...], pair_ref[0, 0, :, :width]]
        value_list = [v_ref[...], pair_ref[0, 0, :, width:]]
        for c in range(opened):
            key_list.append(cut_ref[0, c, :, :width])
            value_list.append(cut_ref[0, c, :, width:])
        dq = jnp.zeros((width, BLOCK), F32)
        for j in range(2 + opened):
            prob = jnp.exp2(dot(key_list[j], query, NT) * factor - lse)
            dscore = (prob * (dot(value_list[j], cot, NT) - delta)).astype(BF16)
            dq = dq + dot(key_list[j], dscore, TN)
            if j == 1:
                continue
            dk = dot(dscore, query, NN) * scale
            dv = dot(prob.astype(BF16), cot, NN)
            if j == 0:
                own_out[0, 0, :, :width] = dk
                own_out[0, 0, :, width:] = dv
            else:
                cut_out[0, j - 2, :, :width] = cut_out[0, j - 2, :, :width] + dk
                cut_out[0, j - 2, :, width:] = cut_out[0, j - 2, :, width:] + dv
        dq_out[...] = (dq * scale).T.astype(BF16)

    for opened in range(1, KCUT + 1):
        pl.when(count[head] == opened)(lambda opened=opened: run(opened))


def backward(slot, count, query, keys, values, pair, cut, cot, stat, heads, width, blocks):
    rows = pl.BlockSpec((BLOCK, width), lambda h, b, s, n: (b, h))
    return pl.pallas_call(
        backward_kernel,
        grid_spec=pltpu.PrefetchScalarGridSpec(
            num_scalar_prefetch=2,
            grid=(heads, blocks),
            in_specs=[
                rows,
                rows,
                rows,
                pl.BlockSpec((1, 1, BLOCK, 2 * width), lambda h, b, s, n: (s[h, b], h, 0, 0)),
                pl.BlockSpec((1, KCUT, BLOCK, 2 * width), lambda h, b, s, n: (h, 0, 0, 0)),
                pl.BlockSpec((1, 1, BLOCK, width), lambda h, b, s, n: (s[h, b], h, 0, 0)),
                pl.BlockSpec((1, 1, 8, BLOCK), lambda h, b, s, n: (s[h, b], h, 0, 0)),
            ],
            out_specs=[
                rows,
                pl.BlockSpec((1, 1, BLOCK, 2 * width), lambda h, b, s, n: (h, b, 0, 0)),
                pl.BlockSpec((1, KCUT, BLOCK, 2 * width), lambda h, b, s, n: (h, 0, 0, 0)),
            ],
        ),
        out_shape=[
            jax.ShapeDtypeStruct((blocks * BLOCK, heads * width), BF16),
            jax.ShapeDtypeStruct((heads, blocks, BLOCK, 2 * width), F32),
            jax.ShapeDtypeStruct((heads, KCUT, BLOCK, 2 * width), F32),
        ],
        compiler_params=params(("arbitrary", "arbitrary")),
        cost_estimate=cost(
            10 * heads * blocks * BLOCK * BLOCK * 6 * width, 12 * blocks * BLOCK * heads * width
        ),
        name="backward",
    )(slot, count, query, keys, values, pair, cut, cot, stat)


def owner_kernel(
    slot, which, k_ref, v_ref, q_ref, cot_ref, stat_ref, own_ref, cut_ref, dk_out, dv_out
):
    width = k_ref.shape[1]
    scale = width ** (-0.5)
    factor = scale * math.log2(math.e)
    query = q_ref[0, 0]
    cot = cot_ref[0, 0]
    prob = jnp.exp2(dot(k_ref[...], query, NT) * factor - stat_ref[0, 0, 0:1, :])
    dscore = (prob * (dot(v_ref[...], cot, NT) - stat_ref[0, 0, 1:2, :])).astype(BF16)
    dk = (dot(dscore, query, NN) * scale).astype(BF16).astype(F32)
    dv = dot(prob.astype(BF16), cot, NN).astype(BF16).astype(F32)
    dk = dk + own_ref[0, 0, :, :width]
    dv = dv + own_ref[0, 0, :, width:]
    c = which[pl.program_id(0), pl.program_id(1)]

    @pl.when(c < 0)
    def _():
        dk_out[...] = dk.astype(BF16)
        dv_out[...] = dv.astype(BF16)

    @pl.when(c >= 0)
    def _():
        place = jnp.maximum(c, 0)
        dk_out[...] = (dk + cut_ref[0, place, :, :width].astype(F32)).astype(BF16)
        dv_out[...] = (dv + cut_ref[0, place, :, width:].astype(F32)).astype(BF16)


def owner(slot, which, keys, values, query, cot, stat, own, cut, heads, width, blocks):
    rows = pl.BlockSpec((BLOCK, width), lambda h, b, s, w: (b, h))
    return pl.pallas_call(
        owner_kernel,
        grid_spec=pltpu.PrefetchScalarGridSpec(
            num_scalar_prefetch=2,
            grid=(heads, blocks),
            in_specs=[
                rows,
                rows,
                pl.BlockSpec((1, 1, BLOCK, width), lambda h, b, s, w: (s[h, b], h, 0, 0)),
                pl.BlockSpec((1, 1, BLOCK, width), lambda h, b, s, w: (s[h, b], h, 0, 0)),
                pl.BlockSpec((1, 1, 8, BLOCK), lambda h, b, s, w: (s[h, b], h, 0, 0)),
                pl.BlockSpec((1, 1, BLOCK, 2 * width), lambda h, b, s, w: (h, b, 0, 0)),
                pl.BlockSpec((1, KCUT, BLOCK, 2 * width), lambda h, b, s, w: (h, 0, 0, 0)),
            ],
            out_specs=[rows, rows],
        ),
        out_shape=[jax.ShapeDtypeStruct((blocks * BLOCK, heads * width), BF16)] * 2,
        compiler_params=params(("arbitrary", "arbitrary")),
        name="owner",
    )(slot, which, keys, values, query, cot, stat, own, cut)


def exchange(x):
    return lax.all_to_all(x, "seq", split_axis=0, concat_axis=0, tiled=True)


def body(query_rows, key_rows, value_rows, out_grad, block_perm, cut_count, norm_gain):
    heads = block_perm.shape[0]
    width = query_rows.shape[1] // heads
    blocks = query_rows.shape[0] // BLOCK
    slots = lax.axis_size("seq")
    features = lax.axis_size("head") * heads * width
    position = lax.axis_index("seq")
    by_dev = block_perm.reshape(heads, slots, blocks)
    local_perm = lax.dynamic_index_in_dim(by_dev, position, 1, keepdims=False)
    recv_slot = local_perm // blocks
    kv_idx = jnp.sum(jnp.where(by_dev // blocks == position, by_dev % blocks, 0), axis=2)
    place = jnp.arange(blocks)
    q_idx = jnp.sum(
        jnp.where(
            recv_slot[:, None, :] == jnp.arange(slots)[None, :, None], place[None, None, :], 0
        ),
        axis=2,
    )
    owned = position * blocks + place
    hits = block_perm[:, None, :] == owned[None, :, None]
    send_slot = jnp.sum(
        jnp.where(hits, (jnp.arange(slots * blocks) // blocks)[None, None, :], 0), axis=2
    )
    cut_global = block_perm[:, :KCUT]
    cut_mine = (cut_global // blocks == position).astype(jnp.int32)
    cut_local = cut_global % blocks
    is_cut = (cut_mine[:, :, None] > 0) & (cut_local[:, :, None] == place[None, None, :])
    which = jnp.sum(jnp.where(is_cut, jnp.arange(1, KCUT + 1)[None, :, None], 0), axis=1) - 1
    gain = norm_gain.reshape(1, heads * width)

    cut_rows = lax.psum(
        cut_pick(cut_local, cut_mine, key_rows, value_rows, heads, width), "seq"
    )
    kv_send, q_send = pack(kv_idx, q_idx, key_rows, value_rows, query_rows, slots, heads, width)
    kv_recv = exchange(kv_send)
    q_recv = exchange(q_send)
    attn, stat = forward(
        recv_slot, cut_count, query_rows, key_rows, value_rows, kv_recv, cut_rows,
        out_grad, gain, heads, width, blocks,
    )
    sums = lax.psum(jnp.sum(stat[:, :, 1:3, :], axis=0), "head")
    scale_row = lax.rsqrt(sums[:, 0] / features + 1e-06)
    coef = scale_row**3 * sums[:, 1] / features
    row = jnp.stack([scale_row, coef], axis=1)
    normed, cot_send, stat_send, gain_part = norm(
        recv_slot, attn, out_grad, gain, stat, row, heads, width, blocks, slots
    )
    cot_recv = exchange(cot_send)
    stat_recv = exchange(stat_send)
    query_grad, own_grad, cut_grad = backward(
        recv_slot, cut_count, query_rows, key_rows, value_rows, kv_recv, cut_rows,
        cot_send, stat_send, heads, width, blocks,
    )
    gain_total = lax.psum(jnp.sum(gain_part, axis=1), "seq")
    cut_total = lax.psum(cut_grad.astype(BF16), "seq")
    key_grad, value_grad = owner(
        send_slot, which, key_rows, value_rows, q_recv, cot_recv, stat_recv, own_grad,
        cut_total, heads, width, blocks,
    )
    return normed, query_grad, key_grad, value_grad, gain_total.reshape(heads * width)


def solution(mesh):
    rows = P("seq", "head")
    return jax.shard_map(
        body,
        mesh=mesh,
        in_specs=(rows, rows, rows, rows, P("head", None), P("head"), P("head")),
        out_specs=(rows, rows, rows, rows, P("head")),
        check_vma=False,
    )
```

time: 686 us -> 371 us (0.54)
  local copies, waits for them, and re-layouts: 173 us -> 17.2 us
  matrix products: 123 us -> 0 us
  other arithmetic: 114 us -> 3.41 us
  Pallas kernels: 0 us -> 76.5 us
  waiting for transfers between devices: 161 us -> 199 us
  blocking collectives: 77.8 us -> 44.1 us
    dot_general x80 -> x0, matrix products: 123 us -> none  [the longest x8 21.5 us: attend(): jnp.einsum('gqd,ckd->gqck', query, cutoff_rows[..., :width], preferred_el...]
    pallas_call x0 -> x6, Pallas kernels: none -> 76.5 us  [the longest x1 27.2 us: backward(): pl.pallas_call(backward_kernel, grid_spec=pltpu.PrefetchScalarGridSpec(nu...]
    reshape x19 -> x1, local copies, waits for them, and re-layouts: 68.5 us -> 0.76 us  [body(): by_dev = block_perm.reshape(heads, slots, blocks)]
    psum x2, waiting for transfers between devices: 104 us -> 151 us  [the longest x1 91.5 us: body(): lax.psum(cut_pick(cut_local, cut_mine, key_rows, value_rows, heads, width...]
    reduce_sum x15 -> x6, other arithmetic: 34.6 us -> 0.61 us  [the longest x1 0.18 us: body(): jnp.sum(jnp.where(hits, (jnp.arange(slots * blocks) // blocks)[None, None...]
    slice x20 -> x0, local copies, waits for them, and re-layouts: 30.4 us -> none  [the longest x8 17.9 us: backward_step(): cut_score = dscore[..., 2 * span:].reshape(2, span, count, span)]
    all_to_all x2 -> x1, blocking collectives: 36.5 us -> 10.7 us  [exchange(): return lax.all_to_all(x, 'seq', split_axis=0, concat_axis=0, tiled=True)]
    convert_element_type x11 -> x1, other arithmetic: 23.7 us -> 2.68 us  [body(): cut_total = lax.psum(cut_grad.astype(BF16), 'seq')]
  transfers between devices with their start and end apart: 6 -> 5, of which waited for: 5 -> 3; matrix products, arithmetic and copies ran while one was open for 7% -> 1% of each run, Pallas kernels for 0% -> 15%
where the time goes in v1:
time: 371 us; the launch traced here: 370 us
  waiting for transfers between devices  199 us (54%)
  Pallas kernels  76.5 us (21%)
  blocking collectives  44.1 us (12%)
  local copies, waits for them, and re-layouts  17.2 us (5%)
  starting transfers between devices  15.4 us (4%)
  between operations  14.2 us (4%)
    psum x1, waiting for transfers between devices, body(): lax.psum(cut_pick(cut_local, cut_mine, key_rows, value_rows, heads, width...  91.5 us
    psum x1, waiting for transfers between devices, body(): cut_total = lax.psum(cut_grad.astype(BF16), 'seq')  59.4 us
    all_to_all x3, waiting for transfers between devices, exchange(): return lax.all_to_all(x, 'seq', split_axis=0, concat_axis=0, tiled=True)  48.3 us
    pallas_call x1, Pallas kernels, backward(): pl.pallas_call(backward_kernel, grid_spec=pltpu.PrefetchScalarGridSpec(nu...  27.2 us
    psum x1, blocking collectives, body(): gain_total = lax.psum(jnp.sum(gain_part, axis=1), 'seq')  22.5 us
    pallas_call x1, Pallas kernels, forward(): pl.pallas_call(forward_kernel, grid_spec=pltpu.PrefetchScalarGridSpec(num...  17.5 us
    unnamed x38, local copies, waits for them, and re-layouts  16.4 us
    all_to_all x3, starting transfers between devices, exchange(): return lax.all_to_all(x, 'seq', split_axis=0, concat_axis=0, tiled=True)  15.3 us
  transfers between devices with their start and end apart: 5, of which 3 were waited for; matrix products, arithmetic and copies ran while one was open for 1% of the time, Pallas kernels for 15%

profile of v1, /device:TPU:0, one launch (start us, length us, event | category | flops | bytes accessed | tf_op | source)
XLA Modules:
  0.0 370.0 jit_solution(1950086873478557105)
XLA Ops:
  8.3 1.2 copy-done
  9.5 1.2 copy-done.2
  10.7 1.2 copy-done.10
  11.9 6.6 %pack.1 = (bf16[8,2,256,256]{3,2,1,0:T(8,128)(2,1)}, bf16[8,2,256,128]{3,2,1,0:T(8,128)(2,1)S(1)}) custom-call(s32[2,8]{1,0:T(2,128)S(1)} %fusion.2.kv_idx, s32[2,8]{1,0:T(2,128)S(1)} %select_reduce_fusion.1.q_idx, bf16[2048,256]{1,0:T(8,128)(2,1)S(1)} %copy-done, bf16[2048,256]{1,0:T(8,128)(2,1)S(1)} %copy-done.2, bf16[2048,256]{1,0:T(8,128)(2,1)S(1)} %copy-done.10), custom_call_target="tpu_custom_call" | custom-call | tf_op jit(solution)/shard_map/pack/pallas_call | solution.py:43
  19.5 7.4 %all-to-all-start = ((bf16[8,2,256,256]{3,2,1,0:T(8,128)(2,1)}), bf16[8,2,256,256]{3,2,1,0:T(8,128)(2,1)}, u32[]{:S(2)}, u32[]{:S(2)}) async-start(bf16[8,2,256,256]{3,2,1,0:T(8,128)(2,1)} %get-tuple-element.18), calls=%async_computation | async-start | bytes 4194304 | tf_op jit(solution)/shard_map/all_to_all | solution.py:356
  26.9 48.3 %all-to-all-done.pair_ref = bf16[8,2,256,256]{3,2,1,0:T(8,128)(2,1)} async-done(((bf16[8,2,256,256]{3,2,1,0:T(8,128)(2,1)}), bf16[8,2,256,256]{3,2,1,0:T(8,128)(2,1)}, u32[]{:S(2)}, u32[]{:S(2)}) %all-to-all-start) | async-done | bytes 2097184 | tf_op jit(solution)/shard_map/all_to_all | solution.py:356
  75.2 3.6 all-to-all-start.1
  79.0 3.6 cut_pick.1
  82.6 91.5 %all-reduce.3.cloned.1.call-done.cut_ref = bf16[2,4,256,256]{3,2,1,0:T(8,128)(2,1)} async-done(((bf16[2,4,256,256]{3,2,1,0:T(8,128)(2,1)}), bf16[2,4,256,256]{3,2,1,0:T(8,128)(2,1)}) %all-reduce.3.cloned.1.call-update) | async-done | bytes 1048592 | tf_op jit(solution)/shard_map/psum | solution.py:389
  174.1 1.2 copy-done.11
  176.6 17.5 %forward.1 = (bf16[2048,256]{1,0:T(8,128)(2,1)S(1)}, f32[2,8,8,256]{3,2,1,0:T(8,128)S(1)}) custom-call(s32[2,8]{1,0:T(2,128)S(1)} %and_select_fusion.4.slot, s32[2]{0:T(128)S(1)} %copy-done.17, bf16[2048,256]{1,0:T(8,128)(2,1)S(1)} %copy-done.11, bf16[2048,256]{1,0:T(8,128)(2,1)S(1)} %copy-done.1, bf16[2048,256]{1,0:T(8,128)(2,1)S(1)} %copy-done.3, ...), custom_call_target="tpu_custom_call" | custom-call | flops 3221225472 | bytes 5242880 | tf_op jit(solution)/shard_map/forward/pallas_call | solution.py:133
  195.1 10.9 %psum.29 = f32[8,2,256]{2,1,0:T(2,128)S(1)} all-reduce(f32[8,2,256]{2,1,0:T(2,128)S(1)} %slice_reduce_fusion), channel_id=1, replica_groups=mesh['seq'=8,'head'=4] {'head'}, use_global_device_ids=true, to_apply=%region_4.5 | all-reduce | flops 4096 | bytes 32768 | tf_op jit(solution)/shard_map/psum | solution.py:399
  208.5 7.9 %norm.1 = (bf16[2048,256]{1,0:T(8,128)(2,1)}, bf16[8,2,256,128]{3,2,1,0:T(8,128)(2,1)S(1)}, f32[8,2,8,256]{3,2,1,0:T(8,128)S(1)}, f32[2,8,128]{2,1,0:T(8,128)S(1)}) custom-call(s32[2,8]{1,0:T(2,128)S(1)} %and_select_fusion.4.slot, bf16[2048,256]{1,0:T(8,128)(2,1)S(1)} %copy-done.6, bf16[2048,256]{1,0:T(8,128)(2,1)S(1)} %copy-done.4, f32[1,256]{1,0:T(1,128)S(1)} %bitcast.5, ...), custom_call_target="tpu_custom_call" | custom-call | tf_op jit(solution)/shard_map/norm/pallas_call | solution.py:195
  217.3 10.7 %all_to_all.20.stat_ref = f32[8,2,8,256]{3,2,1,0:T(8,128)S(1)} all-to-all(f32[8,2,8,256]{3,2,1,0:T(8,128)S(1)} %get-tuple-element.23.stat_ref), channel_id=1, replica_groups=mesh['seq'=8,'head'=4] {'seq'}, dimensions={0} | all-to-all | bytes 262144 | tf_op jit(solution)/shard_map/all_to_all | solution.py:356
  228.0 4.3 %all-to-all-start.2 = ((bf16[8,2,256,128]{3,2,1,0:T(8,128)(2,1)}), bf16[8,2,256,128]{3,2,1,0:T(8,128)(2,1)}, u32[]{:S(2)}, u32[]{:S(2)}) async-start(bf16[8,2,256,128]{3,2,1,0:T(8,128)(2,1)} %copy-done.8), calls=%async_computation.2 | async-start | bytes 2097152 | tf_op jit(solution)/shard_map/all_to_all | solution.py:356
  232.4 1.2 copy-done.9
  233.6 1.2 copy-done.12
  234.8 1.2 copy-done.16
  236.1 27.2 %backward.1 = (bf16[2048,256]{1,0:T(8,128)(2,1)}, f32[2,8,256,256]{3,2,1,0:T(8,128)}, f32[2,4,256,256]{3,2,1,0:T(8,128)}) custom-call(s32[2,8]{1,0:T(2,128)S(1)} %and_select_fusion.4.slot, s32[2]{0:T(128)S(1)} %copy-done.17, bf16[2048,256]{1,0:T(8,128)(2,1)S(1)} %copy-done.12, bf16[2048,256]{1,0:T(8,128)(2,1)S(1)} %copy-done.1, ...), custom_call_target="tpu_custom_call" | custom-call | flops 8053063680 | bytes 6291456 | tf_op jit(solution)/shard_map/backward/pallas_call | solution.py:270
  263.3 2.7 convert_element_type.7
  266.3 22.5 %psum.31 = f32[256]{0:T(256)} all-reduce(f32[256]{0:T(256)S(1)} %bitcast.8), channel_id=1, replica_groups=mesh['seq'=8,'head'=4] {'seq'}, use_global_device_ids=true, to_apply=%region_9.10 | all-reduce | flops 256 | bytes 2048 | tf_op jit(solution)/shard_map/psum | solution.py:412
  288.9 59.4 %all-reduce.5.cloned.1.call-done.cut_ref = bf16[2,4,256,256]{3,2,1,0:T(8,128)(2,1)} async-done(((bf16[2,4,256,256]{3,2,1,0:T(8,128)(2,1)}), bf16[2,4,256,256]{3,2,1,0:T(8,128)(2,1)}) %all-reduce.5.cloned.1.call-update) | async-done | bytes 1048592 | tf_op jit(solution)/shard_map/psum | solution.py:413
  348.3 1.2 copy-done.13
  349.5 13.7 %owner.1 = (bf16[2048,256]{1,0:T(8,128)(2,1)}, bf16[2048,256]{1,0:T(8,128)(2,1)}) custom-call(s32[2,8]{1,0:T(2,128)S(1)} %select_reduce_fusion.slot, s32[2,8]{1,0:T(2,128)S(1)} %broadcast_add_fusion.which, bf16[2048,256]{1,0:T(8,128)(2,1)S(1)} %copy-done.1, bf16[2048,256]{1,0:T(8,128)(2,1)S(1)} %copy-done.3, ...), custom_call_target="tpu_custom_call" | custom-call | tf_op jit(solution)/shard_map/owner/pallas_call | solution.py:333
  (53 shorter events, 8.2 us)
Async XLA Ops:
  8.2 1.2 copy-start
  9.5 1.2 copy-start.2
  10.7 1.2 copy-start.10
  18.5 1.0 copy-start.7
  19.5 7.4 %copy-start.18 = (s32[2,64]{1,0:T(2,128)S(1)}, s32[2,64]{1,0:T(2,128)}, u32[]{:S(2)}) copy-start(s32[2,64]{1,0:T(2,128)} %param.11) | copy-start | bytes 1540
  19.5 55.8 %all-to-all-start = ((bf16[8,2,256,256]{3,2,1,0:T(8,128)(2,1)}), bf16[8,2,256,256]{3,2,1,0:T(8,128)(2,1)}, u32[]{:S(2)}, u32[]{:S(2)}) async-start(bf16[8,2,256,256]{3,2,1,0:T(8,128)(2,1)} %get-tuple-element.18), calls=%async_computation | async-start | bytes 4194304 | tf_op jit(solution)/shard_map/all_to_all | solution.py:356
  26.9 52.0 %copy-start.1 = (bf16[2048,256]{1,0:T(8,128)(2,1)S(1)}, bf16[2048,256]{1,0:T(8,128)(2,1)}, u32[]{:S(2)}) copy-start(bf16[2048,256]{1,0:T(8,128)(2,1)} %k_ref.9) | copy-start | bytes 3145732
  26.9 52.0 %copy-start.3 = (bf16[2048,256]{1,0:T(8,128)(2,1)S(1)}, bf16[2048,256]{1,0:T(8,128)(2,1)}, u32[]{:S(2)}) copy-start(bf16[2048,256]{1,0:T(8,128)(2,1)} %v_ref.9) | copy-start | bytes 3145732
  75.2 142.1 %all-to-all-start.1 = ((bf16[8,2,256,128]{3,2,1,0:T(8,128)(2,1)}), bf16[8,2,256,128]{3,2,1,0:T(8,128)(2,1)S(1)}, u32[]{:S(2)}, u32[]{:S(2)}) async-start(bf16[8,2,256,128]{3,2,1,0:T(8,128)(2,1)} %copy-done.7), calls=%async_computation.1 | async-start | bytes 2097152 | tf_op jit(solution)/shard_map/all_to_all | solution.py:356
  78.9 95.2 %all-reduce.3.cloned.1.call-start = ((), (), s32[]{:S(2)}) async-start(), calls=%async_computation.4 | async-start | bytes 2097152 | tf_op jit(solution)/shard_map/psum | solution.py:389
  79.0 95.2 %copy-start.14 = (f32[256]{0:T(256)S(1)}, f32[256]{0:T(256)}, u32[]{:S(2)}) copy-start(f32[256]{0:T(256)} %param.13) | copy-start | bytes 3076
  79.0 95.1 %copy-start.17 = (s32[2]{0:T(128)S(1)}, s32[2]{0:T(128)}, u32[]{:S(2)}) copy-start(s32[2]{0:T(128)} %count.3) | copy-start | bytes 28
  174.1 1.2 copy-start.11
  175.3 1.2 copy-start.15
  194.1 1.0 copy-start.5
  206.0 1.2 copy-start.4
  207.3 1.2 copy-start.6
  216.4 1.0 copy-start.8
  228.0 120.2 %all-to-all-start.2 = ((bf16[8,2,256,128]{3,2,1,0:T(8,128)(2,1)}), bf16[8,2,256,128]{3,2,1,0:T(8,128)(2,1)}, u32[]{:S(2)}, u32[]{:S(2)}) async-start(bf16[8,2,256,128]{3,2,1,0:T(8,128)(2,1)} %copy-done.8), calls=%async_computation.2 | async-start | bytes 2097152 | tf_op jit(solution)/shard_map/all_to_all | solution.py:356
  232.3 116.0 %all-reduce.5.cloned.1.call-start = ((), (), s32[]{:S(2)}) async-start(), calls=%async_computation.5 | async-start | bytes 2097152 | tf_op jit(solution)/shard_map/psum | solution.py:413
  232.4 1.2 copy-start.9
  233.6 1.2 copy-start.12
  234.8 1.2 copy-start.16
  348.3 1.2 copy-start.13
Sparse Core Ops, SparseCore 0:
  83.8 90.3 all-reduce.2
  266.1 82.1 all-reduce.4

commit v2 on v1

v2 whole, which is shorter than its diff:
```python
import math

import jax
import jax.numpy as jnp
from jax import lax
from jax.experimental import pallas as pl
from jax.experimental.pallas import tpu as pltpu
from jax.sharding import PartitionSpec as P

BLOCK = 256
KCUT = 4
F32 = jnp.float32
BF16 = jnp.bfloat16
NT = (((1,), (1,)), ((), ()))
TN = (((0,), (0,)), ((), ()))
NN = (((1,), (0,)), ((), ()))
VMEM_LIMIT = 48 * 1024 * 1024


def dot(a, b, dims):
    return lax.dot_general(a, b, dims, preferred_element_type=F32)


def params(semantics):
    return pltpu.CompilerParams(
        dimension_semantics=semantics, vmem_limit_bytes=VMEM_LIMIT
    )


def cost(flops, nbytes):
    return pl.CostEstimate(flops=int(flops), bytes_accessed=int(nbytes), transcendentals=0)


EXTRA = 16


def split3(x):
    first = x.astype(BF16)
    rest = x - first.astype(F32)
    second = rest.astype(BF16)
    third = (rest - second.astype(F32)).astype(BF16)
    return [first.astype(F32), second.astype(F32), third.astype(F32)]


def write_stats(ref, values, width):
    pieces = []
    for value in values:
        for piece in split3(value):
            for start in range(0, BLOCK, width):
                pieces.append(piece[:, start : start + width])
    pieces.append(jnp.zeros((EXTRA - len(pieces), width), F32))
    ref[0, 0, BLOCK:, :] = jnp.concatenate(pieces, axis=0).astype(BF16)


def read_stats(ref, width):
    rows = ref[0, 0, BLOCK:, :].astype(F32)
    halves = BLOCK // width
    values = []
    for v in range(2):
        parts = []
        for h in range(halves):
            base = v * 3 * halves + h
            low = rows[base + 2 * halves : base + 2 * halves + 1]
            mid = rows[base + halves : base + halves + 1]
            parts.append(rows[base : base + 1] + (mid + low))
        values.append(jnp.concatenate(parts, axis=1))
    return values


def pack_kernel(kv_idx, q_idx, c_idx, k_ref, v_ref, q_ref, kc_ref, vc_ref, kv_out, q_out, cut_out):
    width = k_ref.shape[1]
    kv_out[0, 0, :, :width] = k_ref[...]
    kv_out[0, 0, :, width:] = v_ref[...]
    q_out[0, 0] = q_ref[...]

    @pl.when(pl.program_id(1) == 0)
    def _():
        cut_out[0, 0, :, :width] = kc_ref[...]
        cut_out[0, 0, :, width:] = vc_ref[...]


def pack(kv_idx, q_idx, c_idx, keys, values, query, slots, heads, width):
    own = pl.BlockSpec((BLOCK, width), lambda h, s, ki, qi, ci: (ki[h, s], h))
    cut = pl.BlockSpec((BLOCK, width), lambda h, s, ki, qi, ci: (ci[h], h))
    return pl.pallas_call(
        pack_kernel,
        grid_spec=pltpu.PrefetchScalarGridSpec(
            num_scalar_prefetch=3,
            grid=(heads, slots),
            in_specs=[
                own,
                own,
                pl.BlockSpec((BLOCK, width), lambda h, s, ki, qi, ci: (qi[h, s], h)),
                cut,
                cut,
            ],
            out_specs=[
                pl.BlockSpec((1, 1, BLOCK, 2 * width), lambda h, s, ki, qi, ci: (s, h, 0, 0)),
                pl.BlockSpec((1, 1, BLOCK, width), lambda h, s, ki, qi, ci: (s, h, 0, 0)),
                pl.BlockSpec((1, 1, BLOCK, 2 * width), lambda h, s, ki, qi, ci: (0, h, 0, 0)),
            ],
        ),
        out_shape=[
            jax.ShapeDtypeStruct((slots, heads, BLOCK, 2 * width), BF16),
            jax.ShapeDtypeStruct((slots, heads, BLOCK, width), BF16),
            jax.ShapeDtypeStruct((1, heads, BLOCK, 2 * width), BF16),
        ],
        compiler_params=params(("arbitrary", "arbitrary")),
        name="pack",
    )(kv_idx, q_idx, c_idx, keys, values, query, keys, values)


def forward_kernel(
    slot, count, dev, q_ref, k_ref, v_ref, pair_ref, cut_ref, g_ref, gain_ref, attn_out, stat_out, s_buf
):
    head = pl.program_id(0)
    width = q_ref.shape[1]
    factor = width ** (-0.5) * math.log2(math.e)

    def run(opened):
        query = q_ref[...]
        key_list = [k_ref[...], pair_ref[0, 0, :, :width]]
        value_list = [v_ref[...], pair_ref[0, 0, :, width:]]
        for c in range(opened):
            key_list.append(cut_ref[dev[head, c], 0, :, :width])
            value_list.append(cut_ref[dev[head, c], 0, :, width:])
        top = None
        for j, piece in enumerate(key_list):
            s = dot(piece, query, NT)
            s_buf[j] = s
            high = jnp.max(s, axis=0, keepdims=True)
            top = high if top is None else jnp.maximum(top, high)
        top = top * factor
        total = jnp.zeros_like(top)
        acc = jnp.zeros((width, BLOCK), F32)
        for j, piece in enumerate(value_list):
            e = jnp.exp2(s_buf[j] * factor - top)
            total = total + jnp.sum(e, axis=0, keepdims=True)
            acc = acc + dot(piece, e.astype(BF16), TN)
        attn_t = (acc / total).astype(BF16).astype(F32)
        attn_out[...] = attn_t.T.astype(BF16)
        grad_t = (g_ref[...].astype(F32) * gain_ref[...]).T
        lse = top + jnp.log2(total)
        square = jnp.sum(attn_t * attn_t, axis=0, keepdims=True)
        mix = jnp.sum(grad_t * attn_t, axis=0, keepdims=True)
        stat_out[0, 0] = jnp.concatenate(
            [lse, square, mix, jnp.zeros((5, BLOCK), F32)], axis=0
        )

    for opened in range(1, KCUT + 1):
        pl.when(count[head] == opened)(lambda opened=opened: run(opened))


def forward(slot, count, dev, query, keys, values, pair, cut, grad, gain, heads, width, blocks):
    rows = pl.BlockSpec((BLOCK, width), lambda h, b, s, n, d: (b, h))
    return pl.pallas_call(
        forward_kernel,
        grid_spec=pltpu.PrefetchScalarGridSpec(
            num_scalar_prefetch=3,
            grid=(heads, blocks),
            in_specs=[
                rows,
                rows,
                rows,
                pl.BlockSpec((1, 1, BLOCK, 2 * width), lambda h, b, s, n, d: (s[h, b], h, 0, 0)),
                pl.BlockSpec((cut.shape[0], 1, BLOCK, 2 * width), lambda h, b, s, n, d: (0, h, 0, 0)),
                rows,
                pl.BlockSpec((1, width), lambda h, b, s, n, d: (0, h)),
            ],
            out_specs=[
                rows,
                pl.BlockSpec((1, 1, 8, BLOCK), lambda h, b, s, n, d: (h, b, 0, 0)),
            ],
            scratch_shapes=[pltpu.VMEM((2 + KCUT, BLOCK, BLOCK), F32)],
        ),
        out_shape=[
            jax.ShapeDtypeStruct((blocks * BLOCK, heads * width), BF16),
            jax.ShapeDtypeStruct((heads, blocks, 8, BLOCK), F32),
        ],
        compiler_params=params(("arbitrary", "arbitrary")),
        cost_estimate=cost(
            4 * heads * blocks * BLOCK * BLOCK * 6 * width, 10 * blocks * BLOCK * heads * width
        ),
        name="forward",
    )(slot, count, dev, query, keys, values, pair, cut, grad, gain)


def norm_kernel(
    slot, attn_ref, g_ref, gain_ref, stat_ref, row_ref, norm_out, cot_out, gain_out, gain_buf
):
    width = attn_ref.shape[1]
    attn = attn_ref[...].astype(F32)
    grad = g_ref[...].astype(F32)
    gain = gain_ref[...]
    scale = jnp.broadcast_to(row_ref[0, 0:1, :], (width, BLOCK)).T
    coef = jnp.broadcast_to(row_ref[0, 1:2, :], (width, BLOCK)).T
    scaled = attn * scale
    norm_out[...] = (scaled * gain).astype(BF16)
    cot = (scale * gain * grad - attn * coef).astype(BF16)
    cot_out[0, 0, :BLOCK, :] = cot
    delta = jnp.sum((cot.astype(F32) * attn).T, axis=0, keepdims=True)
    write_stats(cot_out, [stat_ref[0, 0, 0:1, :], delta], width)
    part = jnp.sum((grad * scaled).reshape(BLOCK // 8, 8, width), axis=0)

    @pl.when(pl.program_id(1) == 0)
    def _():
        gain_buf[...] = part

    @pl.when(pl.program_id(1) > 0)
    def _():
        gain_buf[...] = gain_buf[...] + part

    @pl.when(pl.program_id(1) == pl.num_programs(1) - 1)
    def _():
        pieces = split3(jnp.sum(gain_buf[...], axis=0, keepdims=True))
        pieces.append(jnp.zeros((EXTRA - 3, width), F32))
        gain_out[0] = jnp.concatenate(pieces, axis=0).astype(BF16)


def norm(slot, attn, grad, gain, stat, row, heads, width, blocks, slots):
    rows = pl.BlockSpec((BLOCK, width), lambda h, b, s: (b, h))
    return pl.pallas_call(
        norm_kernel,
        grid_spec=pltpu.PrefetchScalarGridSpec(
            num_scalar_prefetch=1,
            grid=(heads, blocks),
            in_specs=[
                rows,
                rows,
                pl.BlockSpec((1, width), lambda h, b, s: (0, h)),
                pl.BlockSpec((1, 1, 8, BLOCK), lambda h, b, s: (h, b, 0, 0)),
                pl.BlockSpec((1, 2, BLOCK), lambda h, b, s: (b, 0, 0)),
            ],
            out_specs=[
                rows,
                pl.BlockSpec((1, 1, BLOCK + EXTRA, width), lambda h, b, s: (s[h, b], h, 0, 0)),
                pl.BlockSpec((1, EXTRA, width), lambda h, b, s: (h, 0, 0)),
            ],
            scratch_shapes=[pltpu.VMEM((8, width), F32)],
        ),
        out_shape=[
            jax.ShapeDtypeStruct((blocks * BLOCK, heads * width), BF16),
            jax.ShapeDtypeStruct((slots, heads, BLOCK + EXTRA, width), BF16),
            jax.ShapeDtypeStruct((heads, EXTRA, width), BF16),
        ],
        compiler_params=params(("arbitrary", "arbitrary")),
        name="norm",
    )(slot, attn, grad, gain, stat, row)


def cut_kernel(slot, count, dev, q_ref, cut_ref, cot_ref, dq_out, cut_out, sums):
    head = pl.program_id(0)
    step = pl.program_id(1)
    width = q_ref.shape[1]
    scale = width ** (-0.5)
    factor = scale * math.log2(math.e)

    @pl.when(step == 0)
    def _():
        sums[...] = jnp.zeros_like(sums)

    def run(opened):
        query = q_ref[...]
        cot = cot_ref[0, 0, :BLOCK, :]
        lse, delta = read_stats(cot_ref, width)
        dq = jnp.zeros((width, BLOCK), F32)
        for c in range(opened):
            keys = cut_ref[dev[head, c], 0, :, :width]
            values = cut_ref[dev[head, c], 0, :, width:]
            prob = jnp.exp2(dot(keys, query, NT) * factor - lse)
            dscore = (prob * (dot(values, cot, NT) - delta)).astype(BF16)
            dq = dq + dot(keys, dscore, TN)
            sums[c, :, :width] = sums[c, :, :width] + dot(dscore, query, NN) * scale
            sums[c, :, width:] = sums[c, :, width:] + dot(prob.astype(BF16), cot, NN)
        dq_out[0, 0] = dq

    for opened in range(1, KCUT + 1):
        pl.when(count[head] == opened)(lambda opened=opened: run(opened))

    @pl.when(step == pl.num_programs(1) - 1)
    def _():
        cut_out[0] = sums[...].astype(BF16)


def cut_backward(slot, count, dev, query, cut, cot, heads, width, blocks):
    return pl.pallas_call(
        cut_kernel,
        grid_spec=pltpu.PrefetchScalarGridSpec(
            num_scalar_prefetch=3,
            grid=(heads, blocks),
            in_specs=[
                pl.BlockSpec((BLOCK, width), lambda h, b, s, n, d: (b, h)),
                pl.BlockSpec(
                    (cut.shape[0], 1, BLOCK, 2 * width), lambda h, b, s, n, d: (0, h, 0, 0)
                ),
                pl.BlockSpec(
                    (1, 1, BLOCK + EXTRA, width), lambda h, b, s, n, d: (s[h, b], h, 0, 0)
                ),
            ],
            out_specs=[
                pl.BlockSpec((1, 1, width, BLOCK), lambda h, b, s, n, d: (h, b, 0, 0)),
                pl.BlockSpec((1, KCUT, BLOCK, 2 * width), lambda h, b, s, n, d: (h, 0, 0, 0)),
            ],
            scratch_shapes=[pltpu.VMEM((KCUT, BLOCK, 2 * width), F32)],
        ),
        out_shape=[
            jax.ShapeDtypeStruct((heads, blocks, width, BLOCK), F32),
            jax.ShapeDtypeStruct((heads, KCUT, BLOCK, 2 * width), BF16),
        ],
        compiler_params=params(("arbitrary", "arbitrary")),
        cost_estimate=cost(
            40 * heads * blocks * BLOCK * BLOCK * width, 12 * blocks * BLOCK * heads * width
        ),
        name="cut_backward",
    )(slot, count, dev, query, cut, cot)


def near_kernel(
    slot, peer, which, q_ref, k_ref, v_ref, pair_ref, cot_ref, part_ref, far_q, far_cot,
    dq_out, dk_out, dv_out, keep_out,
):
    width = q_ref.shape[1]
    scale = width ** (-0.5)
    factor = scale * math.log2(math.e)
    keys = k_ref[...]
    values = v_ref[...]

    def terms(k, v, query, cot, stats):
        lse, delta = stats
        prob = jnp.exp2(dot(k, query, NT) * factor - lse)
        dscore = (prob * (dot(v, cot, NT) - delta)).astype(BF16)
        return prob.astype(BF16), dscore

    query = q_ref[...]
    cot = cot_ref[0, 0, :BLOCK, :]
    stats = read_stats(cot_ref, width)
    prob, dscore = terms(keys, values, query, cot, stats)
    dq = part_ref[0, 0] + dot(keys, dscore, TN)
    dk = dot(dscore, query, NN) * scale
    dv = dot(prob, cot, NN)
    pair_keys = pair_ref[0, 0, :, :width]
    _, dscore = terms(pair_keys, pair_ref[0, 0, :, width:], query, cot, stats)
    dq = dq + dot(pair_keys, dscore, TN)
    dq_out[...] = (dq * scale).T.astype(BF16)
    query = far_q[0, 0]
    cot = far_cot[0, 0, :BLOCK, :]
    prob, dscore = terms(keys, values, query, cot, read_stats(far_cot, width))
    dk = dk + (dot(dscore, query, NN) * scale).astype(BF16).astype(F32)
    dv = dv + dot(prob, cot, NN).astype(BF16).astype(F32)
    dk_out[...] = dk.astype(BF16)
    dv_out[...] = dv.astype(BF16)

    @pl.when(which[pl.program_id(0)] == pl.program_id(1))
    def _():
        keep_out[0, :, :width] = dk
        keep_out[0, :, width:] = dv


def near(slot, peer, which, query, keys, values, pair, cot, part, far_q, far_cot, heads, width, blocks):
    rows = pl.BlockSpec((BLOCK, width), lambda h, b, s, p, w: (b, h))
    tall = BLOCK + EXTRA
    return pl.pallas_call(
        near_kernel,
        grid_spec=pltpu.PrefetchScalarGridSpec(
            num_scalar_prefetch=3,
            grid=(heads, blocks),
            in_specs=[
                rows,
                rows,
                rows,
                pl.BlockSpec((1, 1, BLOCK, 2 * width), lambda h, b, s, p, w: (s[h, b], h, 0, 0)),
                pl.BlockSpec((1, 1, tall, width), lambda h, b, s, p, w: (s[h, b], h, 0, 0)),
                pl.BlockSpec((1, 1, width, BLOCK), lambda h, b, s, p, w: (h, b, 0, 0)),
                pl.BlockSpec((1, 1, BLOCK, width), lambda h, b, s, p, w: (p[h, b], h, 0, 0)),
                pl.BlockSpec((1, 1, tall, width), lambda h, b, s, p, w: (p[h, b], h, 0, 0)),
            ],
            out_specs=[
                rows,
                rows,
                rows,
                pl.BlockSpec((1, BLOCK, 2 * width), lambda h, b, s, p, w: (h, 0, 0)),
            ],
        ),
        out_shape=[jax.ShapeDtypeStruct((blocks * BLOCK, heads * width), BF16)] * 3
        + [jax.ShapeDtypeStruct((heads, BLOCK, 2 * width), F32)],
        compiler_params=params(("arbitrary", "arbitrary")),
        cost_estimate=cost(
            50 * heads * blocks * BLOCK * BLOCK * width, 24 * blocks * BLOCK * heads * width
        ),
        name="near",
    )(slot, peer, which, query, keys, values, pair, cot, part, far_q, far_cot)


def patch_kernel(index, term, has, keep_ref, cut_ref, dk_ref, dv_ref, dk_out, dv_out):
    width = dk_ref.shape[1]
    flag = has[pl.program_id(0)] > 0
    total = keep_ref[0] + cut_ref[0, 0].astype(F32)
    dk_out[...] = jnp.where(flag, total[:, :width].astype(BF16), dk_ref[...])
    dv_out[...] = jnp.where(flag, total[:, width:].astype(BF16), dv_ref[...])


def patch(index, term, has, keep, cut, key_grad, value_grad, heads, width):
    rows = pl.BlockSpec((BLOCK, width), lambda h, i, t, f: (i[h], h))
    return pl.pallas_call(
        patch_kernel,
        grid_spec=pltpu.PrefetchScalarGridSpec(
            num_scalar_prefetch=3,
            grid=(heads,),
            in_specs=[
                pl.BlockSpec((1, BLOCK, 2 * width), lambda h, i, t, f: (h, 0, 0)),
                pl.BlockSpec((1, 1, BLOCK, 2 * width), lambda h, i, t, f: (h, t[h], 0, 0)),
                rows,
                rows,
            ],
            out_specs=[rows, rows],
        ),
        out_shape=[jax.ShapeDtypeStruct(key_grad.shape, BF16)] * 2,
        input_output_aliases={5: 0, 6: 1},
        compiler_params=params(("arbitrary",)),
        name="patch",
    )(index, term, has, keep, cut, key_grad, value_grad)


def exchange(x):
    return lax.all_to_all(x, "seq", split_axis=0, concat_axis=0, tiled=True)


def body(query_rows, key_rows, value_rows, out_grad, block_perm, cut_count, norm_gain):
    heads = block_perm.shape[0]
    width = query_rows.shape[1] // heads
    blocks = query_rows.shape[0] // BLOCK
    slots = lax.axis_size("seq")
    features = lax.axis_size("head") * heads * width
    position = lax.axis_index("seq")
    by_dev = block_perm.reshape(heads, slots, blocks)
    local_perm = lax.dynamic_index_in_dim(by_dev, position, 1, keepdims=False)
    recv_slot = local_perm // blocks
    kv_idx = jnp.sum(jnp.where(by_dev // blocks == position, by_dev % blocks, 0), axis=2)
    place = jnp.arange(blocks)
    q_idx = jnp.sum(
        jnp.where(
            recv_slot[:, None, :] == jnp.arange(slots)[None, :, None], place[None, None, :], 0
        ),
        axis=2,
    )
    owned = position * blocks + place
    hits = block_perm[:, None, :] == owned[None, :, None]
    send_slot = jnp.sum(
        jnp.where(hits, (jnp.arange(slots * blocks) // blocks)[None, None, :], 0), axis=2
    )
    cut_global = block_perm[:, :KCUT]
    cut_dev = cut_global // blocks
    cut_mine = cut_dev == position
    cut_has = jnp.sum(cut_mine.astype(jnp.int32), axis=1)
    cut_local = jnp.sum(jnp.where(cut_mine, cut_global % blocks, 0), axis=1)
    cut_term = jnp.sum(jnp.where(cut_mine, jnp.arange(KCUT)[None, :], 0), axis=1)
    gain = norm_gain.reshape(1, heads * width)

    kv_send, q_send, cut_send = pack(
        kv_idx, q_idx, cut_local, key_rows, value_rows, query_rows, slots, heads, width
    )
    cut_rows = lax.all_gather(cut_send, "seq", axis=0, tiled=True)
    kv_recv = exchange(kv_send)
    q_send, kv_recv, cut_rows = lax.optimization_barrier((q_send, kv_recv, cut_rows))
    q_recv = exchange(q_send)
    attn, stat = forward(
        recv_slot, cut_count, cut_dev, query_rows, key_rows, value_rows, kv_recv, cut_rows,
        out_grad, gain, heads, width, blocks,
    )
    sums = lax.psum(jnp.sum(stat[:, :, 1:3, :], axis=0), "head")
    scale_row = lax.rsqrt(sums[:, 0] / features + 1e-06)
    coef = scale_row**3 * sums[:, 1] / features
    row = jnp.stack([scale_row, coef], axis=1)
    normed, cot_send, gain_part = norm(
        recv_slot, attn, out_grad, gain, stat, row, heads, width, blocks, slots
    )
    cot_recv = exchange(cot_send)
    dq_part, cut_part = cut_backward(
        recv_slot, cut_count, cut_dev, query_rows, cut_rows, cot_send, heads, width, blocks
    )
    shares = exchange(cut_part.reshape(slots, heads * KCUT * BLOCK // slots, 2 * width))
    query_grad, key_grad, value_grad, keep = near(
        recv_slot, send_slot, cut_local, query_rows, key_rows, value_rows, kv_recv, cot_send,
        dq_part, q_recv, cot_recv, heads, width, blocks,
    )
    share = jnp.sum(shares.astype(F32), axis=0).astype(BF16)
    depth = share.shape[0]
    tail = jnp.concatenate([share, gain_part.reshape(-1, 2 * width)], axis=0)
    gathered = lax.all_gather(tail, "seq", axis=0)
    cut_total = gathered[:, :depth].reshape(heads, KCUT, BLOCK, 2 * width)
    gain_total = jnp.sum(
        gathered[:, depth:].reshape(slots, heads, EXTRA, width).astype(F32), axis=(0, 2)
    )
    key_grad, value_grad = patch(
        cut_local, cut_term, cut_has, keep, cut_total, key_grad, value_grad, heads, width
    )
    return normed, query_grad, key_grad, value_grad, gain_total.reshape(heads * width)


def solution(mesh):
    rows = P("seq", "head")
    return jax.shard_map(
        body,
        mesh=mesh,
        in_specs=(rows, rows, rows, rows, P("head", None), P("head"), P("head")),
        out_specs=(rows, rows, rows, rows, P("head")),
        check_vma=False,
    )
```

time: 371 us -> 273 us (0.74)
  waiting for transfers between devices: 199 us -> 103 us
  blocking collectives: 44.1 us -> 39.5 us
    psum x2 -> x0, waiting for transfers between devices: 151 us -> none  [the longest x1 91.5 us: body(): lax.psum(cut_pick(cut_local, cut_mine, key_rows, value_rows, heads, width...]
    all_gather x0 -> x2, waiting for transfers between devices: none -> 75 us  [the longest x1 75 us: body(): cut_rows = lax.all_gather(cut_send, 'seq', axis=0, tiled=True)]
    psum x1 -> x0, blocking collectives: 22.5 us -> none  [body(): gain_total = lax.psum(jnp.sum(gain_part, axis=1), 'seq')]
    all_to_all x3, waiting for transfers between devices: 48.3 us -> 27.9 us  [exchange(): return lax.all_to_all(x, 'seq', split_axis=0, concat_axis=0, tiled=True)]
    all_to_all x1, blocking collectives: 10.7 us -> 29.3 us  [exchange(): return lax.all_to_all(x, 'seq', split_axis=0, concat_axis=0, tiled=True)]
    unnamed x38 -> x36, local copies, waits for them, and re-layouts: 16.4 us -> 12.4 us
  transfers between devices with their start and end apart: 5 -> 5, of which waited for: 3 -> 2; matrix products, arithmetic and copies ran while one was open for 1% -> 1% of each run, Pallas kernels for 15% -> 26%
where the time goes in v2:
time: 273 us
  waiting for transfers between devices  103 us (38%)
  Pallas kernels  79.7 us (29%)
  blocking collectives  39.5 us (14%)
  starting transfers between devices  16.1 us (6%)
  local copies, waits for them, and re-layouts  14.4 us (5%)
  between operations  14.3 us (5%)
  other arithmetic  5.51 us (2%)
    all_gather x1, waiting for transfers between devices, body(): cut_rows = lax.all_gather(cut_send, 'seq', axis=0, tiled=True)  75 us
    all_to_all x1, blocking collectives, exchange(): return lax.all_to_all(x, 'seq', split_axis=0, concat_axis=0, tiled=True)  29.3 us
    all_to_all x3, waiting for transfers between devices, exchange(): return lax.all_to_all(x, 'seq', split_axis=0, concat_axis=0, tiled=True)  27.9 us
    pallas_call x1, Pallas kernels, cut_backward(): pl.pallas_call(cut_kernel, grid_spec=pltpu.PrefetchScalarGridSpec(num_sca...  22.1 us
    pallas_call x1, Pallas kernels, near(): pl.pallas_call(near_kernel, grid_spec=pltpu.PrefetchScalarGridSpec(num_sc...  20 us
    pallas_call x1, Pallas kernels, forward(): pl.pallas_call(forward_kernel, grid_spec=pltpu.PrefetchScalarGridSpec(num...  20 us
    all_to_all x3, starting transfers between devices, exchange(): return lax.all_to_all(x, 'seq', split_axis=0, concat_axis=0, tiled=True)  16 us
    unnamed x36, local copies, waits for them, and re-layouts  12.4 us
  transfers between devices with their start and end apart: 5, of which 2 were waited for; matrix products, arithmetic and copies ran while one was open for 1% of the time, Pallas kernels for 26%

profile of v2, /device:TPU:0, one launch (start us, length us, event | category | flops | bytes accessed | tf_op | source)
XLA Modules:
  0.0 272.6 jit_solution(13674354665119227920)
XLA Ops:
  9.7 1.2 copy-done
  10.9 1.2 copy-done.2
  12.1 1.2 copy-done.4
  13.4 7.1 %pack.1 = (bf16[8,2,256,256]{3,2,1,0:T(8,128)(2,1)}, bf16[8,2,256,128]{3,2,1,0:T(8,128)(2,1)S(1)}, bf16[1,2,256,256]{3,2,1,0:T(8,128)(2,1)}) custom-call(s32[2,8]{1,0:T(2,128)S(1)} %get-tuple-element.52.kv_idx, s32[2,8]{1,0:T(2,128)S(1)} %get-tuple-element.53.q_idx, s32[2]{0:T(128)S(1)} %get-tuple-element.45.c_idx.which.index, ...), custom_call_target="tpu_custom_call" | custom-call | tf_op jit(solution)/shard_map/pack/pallas_call | solution.py:85
  20.4 1.0 copy-done.10
  21.4 7.4 %all-to-all-start = ((bf16[8,2,256,256]{3,2,1,0:T(8,128)(2,1)}), bf16[8,2,256,256]{3,2,1,0:T(8,128)(2,1)}, u32[]{:S(2)}, u32[]{:S(2)}) async-start(bf16[8,2,256,256]{3,2,1,0:T(8,128)(2,1)} %get-tuple-element.25), calls=%async_computation | async-start | bytes 4194304 | tf_op jit(solution)/shard_map/all_to_all | solution.py:425
  28.9 75.0 %all-gather.4.cloned.1.call-done.cut_ref = bf16[8,2,256,256]{3,2,1,0:T(8,128)(2,1)} async-done(((bf16[1,2,256,256]{3,2,1,0:T(8,128)(2,1)}), bf16[8,2,256,256]{3,2,1,0:T(8,128)(2,1)}) %all-gather.4.cloned.1.call-update) | async-done | bytes 2097168 | tf_op jit(solution)/shard_map/all_gather | solution.py:462
  103.9 4.2 %all-to-all-start.1 = ((bf16[8,2,256,128]{3,2,1,0:T(8,128)(2,1)}), bf16[8,2,256,128]{3,2,1,0:T(8,128)(2,1)}, u32[]{:S(2)}, u32[]{:S(2)}) async-start(bf16[8,2,256,128]{3,2,1,0:T(8,128)(2,1)} %copy-done.10), calls=%async_computation.1 | async-start | bytes 2097152 | tf_op jit(solution)/shard_map/all_to_all | solution.py:425
  108.2 1.2 copy-done.6
  109.5 20.0 %forward.1 = (bf16[2048,256]{1,0:T(8,128)(2,1)S(1)}, f32[2,8,8,256]{3,2,1,0:T(8,128)S(1)}) custom-call(s32[2,8]{1,0:T(2,128)S(1)} %and_select_fusion.4.slot, s32[2]{0:T(128)S(1)} %copy-done.15, s32[2,4]{1,0:T(2,128)S(1)} %get-tuple-element.49.dev, bf16[2048,256]{1,0:T(8,128)(2,1)S(1)} %copy-done.5, bf16[2048,256]{1,0:T(8,128)(2,1)S(1)} %copy-done.1, ...), custom_call_target="tpu_custom_call" | custom-call | flops 3221225472 | bytes 5242880 | tf_op jit(solution)/shard_map/forward/pallas_call | solution.py:156
  129.5 1.0 copy-done.8
  130.5 10.2 %psum.7 = f32[8,2,256]{2,1,0:T(2,128)S(1)} all-reduce(f32[8,2,256]{2,1,0:T(2,128)S(1)} %slice_reduce_fusion), channel_id=1, replica_groups=mesh['seq'=8,'head'=4] {'head'}, use_global_device_ids=true, to_apply=%region_4.5 | all-reduce | flops 4096 | bytes 32768 | tf_op jit(solution)/shard_map/psum | solution.py:470
  140.8 1.2 copy-done.7
  142.0 1.2 copy-done.9
  143.2 8.2 %norm.1 = (bf16[2048,256]{1,0:T(8,128)(2,1)}, bf16[8,2,272,128]{3,2,1,0:T(8,128)(2,1)}, bf16[2,16,128]{2,1,0:T(8,128)(2,1)S(1)}) custom-call(s32[2,8]{1,0:T(2,128)S(1)} %and_select_fusion.4.slot, bf16[2048,256]{1,0:T(8,128)(2,1)S(1)} %copy-done.9, bf16[2048,256]{1,0:T(8,128)(2,1)S(1)} %copy-done.7, f32[1,256]{1,0:T(1,128)S(1)} %bitcast.10, ...), custom_call_target="tpu_custom_call" | custom-call | tf_op jit(solution)/shard_map/norm/pallas_call | solution.py:222
  151.5 22.1 %cut_backward.1 = (f32[2,8,128,256]{3,2,1,0:T(8,128)S(1)}, bf16[2,4,256,256]{3,2,1,0:T(8,128)(2,1)S(1)}) custom-call(s32[2,8]{1,0:T(2,128)S(1)} %and_select_fusion.4.slot, s32[2]{0:T(128)S(1)} %copy-done.15, s32[2,4]{1,0:T(2,128)S(1)} %get-tuple-element.49.dev, bf16[2048,256]{1,0:T(8,128)(2,1)S(1)} %copy-done.5, ...), custom_call_target="tpu_custom_call" | custom-call | flops 5368709120 | bytes 6291456 | tf_op jit(solution)/shard_map/cut_backward/pallas_call | solution.py:286
  174.6 1.3 copy-done.16
  175.9 29.3 %all_to_all.20 = bf16[8,256,256]{2,1,0:T(8,128)(2,1)} all-to-all(bf16[8,256,256]{2,1,0:T(8,128)(2,1)} %bitcast.8), channel_id=1, replica_groups=mesh['seq'=8,'head'=4] {'seq'}, dimensions={0} | all-to-all | bytes 2097152 | tf_op jit(solution)/shard_map/all_to_all | solution.py:425
  205.2 4.4 %all-to-all-start.2 = ((bf16[8,2,272,128]{3,2,1,0:T(8,128)(2,1)}), bf16[8,2,272,128]{3,2,1,0:T(8,128)(2,1)}, u32[]{:S(2)}, u32[]{:S(2)}) async-start(bf16[8,2,272,128]{3,2,1,0:T(8,128)(2,1)} %get-tuple-element.32.cot_ref), calls=%async_computation.2 | async-start | bytes 2228224 | tf_op jit(solution)/shard_map/all_to_all | solution.py:425
  209.6 1.4 reduce_sum.98
  211.9 27.9 %all-to-all-done.2.far_cot = bf16[8,2,272,128]{3,2,1,0:T(8,128)(2,1)} async-done(((bf16[8,2,272,128]{3,2,1,0:T(8,128)(2,1)}), bf16[8,2,272,128]{3,2,1,0:T(8,128)(2,1)}, u32[]{:S(2)}, u32[]{:S(2)}) %all-to-all-start.2) | async-done | bytes 1114144 | tf_op jit(solution)/shard_map/all_to_all | solution.py:425
  239.9 20.0 %near.1 = (bf16[2048,256]{1,0:T(8,128)(2,1)}, bf16[2048,256]{1,0:T(8,128)(2,1)}, bf16[2048,256]{1,0:T(8,128)(2,1)}, f32[2,256,256]{2,1,0:T(8,128)S(1)}) custom-call(s32[2,8]{1,0:T(2,128)S(1)} %and_select_fusion.4.slot, s32[2,8]{1,0:T(2,128)S(1)} %select_reduce_fusion.peer, s32[2]{0:T(128)S(1)} %get-tuple-element.45.c_idx.which.index, ...), custom_call_target="tpu_custom_call" | custom-call | flops 6710886400 | bytes 12582912 | tf_op jit(solution)/shard_map/near/pallas_call | solution.py:362
  261.6 1.3 slice.26
  263.5 2.2 patch.1
  (51 shorter events, 6.8 us)
Async XLA Ops:
  7.2 96.8 %all-gather.4.cloned.1.call-start = ((), (), s32[]{:S(2)}) async-start(), calls=%async_computation.4 | async-start | bytes 2359296 | tf_op jit(solution)/shard_map/all_gather | solution.py:462
  9.7 1.2 copy-start
  10.9 1.2 copy-start.2
  12.1 1.2 copy-start.4
  20.4 1.0 copy-start.10
  21.4 86.8 %copy-start.5 = (bf16[2048,256]{1,0:T(8,128)(2,1)S(1)}, bf16[2048,256]{1,0:T(8,128)(2,1)}, u32[]{:S(2)}) copy-start(bf16[2048,256]{1,0:T(8,128)(2,1)} %q_ref.7) | copy-start | bytes 3145732
  21.4 82.5 %all-to-all-start = ((bf16[8,2,256,256]{3,2,1,0:T(8,128)(2,1)}), bf16[8,2,256,256]{3,2,1,0:T(8,128)(2,1)}, u32[]{:S(2)}, u32[]{:S(2)}) async-start(bf16[8,2,256,256]{3,2,1,0:T(8,128)(2,1)} %get-tuple-element.25), calls=%async_computation | async-start | bytes 4194304 | tf_op jit(solution)/shard_map/all_to_all | solution.py:425
  28.9 79.3 %copy-start.1 = (bf16[2048,256]{1,0:T(8,128)(2,1)S(1)}, bf16[2048,256]{1,0:T(8,128)(2,1)}, u32[]{:S(2)}) copy-start(bf16[2048,256]{1,0:T(8,128)(2,1)} %k_ref.5) | copy-start | bytes 3145732
  28.9 79.4 %copy-start.3 = (bf16[2048,256]{1,0:T(8,128)(2,1)S(1)}, bf16[2048,256]{1,0:T(8,128)(2,1)}, u32[]{:S(2)}) copy-start(bf16[2048,256]{1,0:T(8,128)(2,1)} %v_ref.5) | copy-start | bytes 3145732
  28.9 79.3 %copy-start.14 = (f32[256]{0:T(256)S(1)}, f32[256]{0:T(256)}, u32[]{:S(2)}) copy-start(f32[256]{0:T(256)} %param.13) | copy-start | bytes 3076
  28.9 79.3 %copy-start.15 = (s32[2]{0:T(128)S(1)}, s32[2]{0:T(128)}, u32[]{:S(2)}) copy-start(s32[2]{0:T(128)} %count.3) | copy-start | bytes 28
  103.9 71.9 %all-to-all-start.1 = ((bf16[8,2,256,128]{3,2,1,0:T(8,128)(2,1)}), bf16[8,2,256,128]{3,2,1,0:T(8,128)(2,1)}, u32[]{:S(2)}, u32[]{:S(2)}) async-start(bf16[8,2,256,128]{3,2,1,0:T(8,128)(2,1)} %copy-done.10), calls=%async_computation.1 | async-start | bytes 2097152 | tf_op jit(solution)/shard_map/all_to_all | solution.py:425
  108.2 1.2 copy-start.6
  129.5 1.0 copy-start.8
  140.8 1.2 copy-start.7
  142.0 1.2 copy-start.9
  173.6 1.0 copy-start.11
  174.6 1.3 copy-start.16
  205.2 6.6 %copy-start.17 = (s32[2,64]{1,0:T(2,128)S(1)}, s32[2,64]{1,0:T(2,128)}, u32[]{:S(2)}) copy-start(s32[2,64]{1,0:T(2,128)} %param.11) | copy-start | bytes 1540
  205.2 34.7 %all-to-all-start.2 = ((bf16[8,2,272,128]{3,2,1,0:T(8,128)(2,1)}), bf16[8,2,272,128]{3,2,1,0:T(8,128)(2,1)}, u32[]{:S(2)}, u32[]{:S(2)}) async-start(bf16[8,2,272,128]{3,2,1,0:T(8,128)(2,1)} %get-tuple-element.32.cot_ref), calls=%async_computation.2 | async-start | bytes 2228224 | tf_op jit(solution)/shard_map/all_to_all | solution.py:425
  209.6 51.1 %all-gather.6.cloned.1.call-start = ((), (), s32[]{:S(2)}) async-start(), calls=%async_computation.5 | async-start | bytes 1253376 | tf_op jit(solution)/shard_map/all_gather | solution.py:489
  259.9 0.8 copy-start.12
  260.7 2.8 %copy-start.13 = (f32[2,256,256]{2,1,0:T(8,128)S(1)}, f32[2,256,256]{2,1,0:T(8,128)}, u32[]{:S(2)}) copy-start(f32[2,256,256]{2,1,0:T(8,128)} %copy-done.12) | copy-start | bytes 1572868
Sparse Core Ops, SparseCore 0:
  21.5 82.3 all-gather.3
  212.6 46.1 all-gather.5

commit v3 on v2

--- a/solution.py
+++ b/solution.py
@@ -6,6 +6,7 @@
 from jax.experimental import pallas as pl
 from jax.experimental.pallas import tpu as pltpu
 from jax.sharding import PartitionSpec as P
+
 
 BLOCK = 256
 KCUT = 4
@@ -421,7 +422,7 @@
     )(index, term, has, keep, cut, key_grad, value_grad)
 
 
-def exchange(x):
+def exchange_slots(x):
     return lax.all_to_all(x, "seq", split_axis=0, concat_axis=0, tiled=True)
 
 
@@ -460,9 +461,9 @@
         kv_idx, q_idx, cut_local, key_rows, value_rows, query_rows, slots, heads, width
     )
     cut_rows = lax.all_gather(cut_send, "seq", axis=0, tiled=True)
-    kv_recv = exchange(kv_send)
+    kv_recv = exchange_slots(kv_send)
     q_send, kv_recv, cut_rows = lax.optimization_barrier((q_send, kv_recv, cut_rows))
-    q_recv = exchange(q_send)
+    q_recv = exchange_slots(q_send)
     attn, stat = forward(
         recv_slot, cut_count, cut_dev, query_rows, key_rows, value_rows, kv_recv, cut_rows,
         out_grad, gain, heads, width, blocks,
@@ -474,11 +475,11 @@
     normed, cot_send, gain_part = norm(
         recv_slot, attn, out_grad, gain, stat, row, heads, width, blocks, slots
     )
-    cot_recv = exchange(cot_send)
+    cot_recv = exchange_slots(cot_send)
     dq_part, cut_part = cut_backward(
         recv_slot, cut_count, cut_dev, query_rows, cut_rows, cot_send, heads, width, blocks
     )
-    shares = exchange(cut_part.reshape(slots, heads * KCUT * BLOCK // slots, 2 * width))
+    shares = exchange_slots(cut_part.reshape(slots, heads * KCUT * BLOCK // slots, 2 * width))
     query_grad, key_grad, value_grad, keep = near(
         recv_slot, send_slot, cut_local, query_rows, key_rows, value_rows, kv_recv, cot_send,
         dq_part, q_recv, cot_recv, heads, width, blocks,

time: 273 us -> 272 us (level)
  Pallas kernels: 79.7 us -> 76.3 us
  transfers between devices with their start and end apart: 5 -> 5, of which waited for: 2 -> 2; matrix products, arithmetic and copies ran while one was open for 1% -> 1% of each run, Pallas kernels for 26% -> 25%
where the time goes in v3:
time: 272 us; the launch traced here: 271 us
  waiting for transfers between devices  104 us (38%)
  Pallas kernels  76.3 us (28%)
  blocking collectives  40.6 us (15%)
  starting transfers between devices  16.1 us (6%)
  local copies, waits for them, and re-layouts  14.4 us (5%)
  between operations  14.3 us (5%)
  other arithmetic  5.51 us (2%)
    all_gather x1, waiting for transfers between devices, body(): cut_rows = lax.all_gather(cut_send, 'seq', axis=0, tiled=True)  75 us
    all_to_all x1, blocking collectives, exchange_slots(): return lax.all_to_all(x, 'seq', split_axis=0, concat_axis=0, tiled=True)  30 us
    all_to_all x3, waiting for transfers between devices, exchange_slots(): return lax.all_to_all(x, 'seq', split_axis=0, concat_axis=0, tiled=True)  28.5 us
    pallas_call x1, Pallas kernels, near(): pl.pallas_call(near_kernel, grid_spec=pltpu.PrefetchScalarGridSpec(num_sc...  20 us
    pallas_call x1, Pallas kernels, cut_backward(): pl.pallas_call(cut_kernel, grid_spec=pltpu.PrefetchScalarGridSpec(num_sca...  19.9 us
    pallas_call x1, Pallas kernels, forward(): pl.pallas_call(forward_kernel, grid_spec=pltpu.PrefetchScalarGridSpec(num...  18.9 us
    all_to_all x3, starting transfers between devices, exchange_slots(): return lax.all_to_all(x, 'seq', split_axis=0, concat_axis=0, tiled=True)  16 us
    unnamed x36, local copies, waits for them, and re-layouts  12.4 us
  transfers between devices with their start and end apart: 5, of which 2 were waited for; matrix products, arithmetic and copies ran while one was open for 1% of the time, Pallas kernels for 25%

profile of v3, /device:TPU:0, one launch (start us, length us, event | category | flops | bytes accessed | tf_op | source)
XLA Modules:
  0.0 270.8 jit_solution(13674354665119227920)
XLA Ops:
  9.7 1.2 copy-done
  10.9 1.2 copy-done.2
  12.1 1.2 copy-done.4
  13.4 7.1 %pack.1 = (bf16[8,2,256,256]{3,2,1,0:T(8,128)(2,1)}, bf16[8,2,256,128]{3,2,1,0:T(8,128)(2,1)S(1)}, bf16[1,2,256,256]{3,2,1,0:T(8,128)(2,1)}) custom-call(s32[2,8]{1,0:T(2,128)S(1)} %get-tuple-element.52.kv_idx, s32[2,8]{1,0:T(2,128)S(1)} %get-tuple-element.53.q_idx, s32[2]{0:T(128)S(1)} %get-tuple-element.45.c_idx.which.index, ...), custom_call_target="tpu_custom_call" | custom-call | tf_op jit(solution)/shard_map/pack/pallas_call | solution.py:86
  20.4 1.0 copy-done.10
  21.4 7.4 %all-to-all-start = ((bf16[8,2,256,256]{3,2,1,0:T(8,128)(2,1)}), bf16[8,2,256,256]{3,2,1,0:T(8,128)(2,1)}, u32[]{:S(2)}, u32[]{:S(2)}) async-start(bf16[8,2,256,256]{3,2,1,0:T(8,128)(2,1)} %get-tuple-element.25), calls=%async_computation | async-start | bytes 4194304 | tf_op jit(solution)/shard_map/all_to_all | solution.py:426
  28.9 75.0 %all-gather.4.cloned.1.call-done.cut_ref = bf16[8,2,256,256]{3,2,1,0:T(8,128)(2,1)} async-done(((bf16[1,2,256,256]{3,2,1,0:T(8,128)(2,1)}), bf16[8,2,256,256]{3,2,1,0:T(8,128)(2,1)}) %all-gather.4.cloned.1.call-update) | async-done | bytes 2097168 | tf_op jit(solution)/shard_map/all_gather | solution.py:463
  103.9 4.2 %all-to-all-start.1 = ((bf16[8,2,256,128]{3,2,1,0:T(8,128)(2,1)}), bf16[8,2,256,128]{3,2,1,0:T(8,128)(2,1)}, u32[]{:S(2)}, u32[]{:S(2)}) async-start(bf16[8,2,256,128]{3,2,1,0:T(8,128)(2,1)} %copy-done.10), calls=%async_computation.1 | async-start | bytes 2097152 | tf_op jit(solution)/shard_map/all_to_all | solution.py:426
  108.2 1.2 copy-done.6
  109.5 18.9 %forward.1 = (bf16[2048,256]{1,0:T(8,128)(2,1)S(1)}, f32[2,8,8,256]{3,2,1,0:T(8,128)S(1)}) custom-call(s32[2,8]{1,0:T(2,128)S(1)} %and_select_fusion.4.slot, s32[2]{0:T(128)S(1)} %copy-done.15, s32[2,4]{1,0:T(2,128)S(1)} %get-tuple-element.49.dev, bf16[2048,256]{1,0:T(8,128)(2,1)S(1)} %copy-done.5, bf16[2048,256]{1,0:T(8,128)(2,1)S(1)} %copy-done.1, ...), custom_call_target="tpu_custom_call" | custom-call | flops 3221225472 | bytes 5242880 | tf_op jit(solution)/shard_map/forward/pallas_call | solution.py:157
  129.4 10.5 %psum.7 = f32[8,2,256]{2,1,0:T(2,128)S(1)} all-reduce(f32[8,2,256]{2,1,0:T(2,128)S(1)} %slice_reduce_fusion), channel_id=1, replica_groups=mesh['seq'=8,'head'=4] {'head'}, use_global_device_ids=true, to_apply=%region_4.5 | all-reduce | flops 4096 | bytes 32768 | tf_op jit(solution)/shard_map/psum | solution.py:471
  139.9 1.2 copy-done.7
  141.2 1.2 copy-done.9
  142.4 8.2 %norm.1 = (bf16[2048,256]{1,0:T(8,128)(2,1)}, bf16[8,2,272,128]{3,2,1,0:T(8,128)(2,1)}, bf16[2,16,128]{2,1,0:T(8,128)(2,1)S(1)}) custom-call(s32[2,8]{1,0:T(2,128)S(1)} %and_select_fusion.4.slot, bf16[2048,256]{1,0:T(8,128)(2,1)S(1)} %copy-done.9, bf16[2048,256]{1,0:T(8,128)(2,1)S(1)} %copy-done.7, f32[1,256]{1,0:T(1,128)S(1)} %bitcast.10, ...), custom_call_target="tpu_custom_call" | custom-call | tf_op jit(solution)/shard_map/norm/pallas_call | solution.py:223
  150.6 19.9 %cut_backward.1 = (f32[2,8,128,256]{3,2,1,0:T(8,128)S(1)}, bf16[2,4,256,256]{3,2,1,0:T(8,128)(2,1)S(1)}) custom-call(s32[2,8]{1,0:T(2,128)S(1)} %and_select_fusion.4.slot, s32[2]{0:T(128)S(1)} %copy-done.15, s32[2,4]{1,0:T(2,128)S(1)} %get-tuple-element.49.dev, bf16[2048,256]{1,0:T(8,128)(2,1)S(1)} %copy-done.5, ...), custom_call_target="tpu_custom_call" | custom-call | flops 5368709120 | bytes 6291456 | tf_op jit(solution)/shard_map/cut_backward/pallas_call | solution.py:287
  170.5 1.0 copy-done.11
  171.5 1.3 copy-done.16
  172.8 30.0 %all_to_all.20 = bf16[8,256,256]{2,1,0:T(8,128)(2,1)} all-to-all(bf16[8,256,256]{2,1,0:T(8,128)(2,1)} %bitcast.8), channel_id=1, replica_groups=mesh['seq'=8,'head'=4] {'seq'}, dimensions={0} | all-to-all | bytes 2097152 | tf_op jit(solution)/shard_map/all_to_all | solution.py:426
  202.8 4.4 %all-to-all-start.2 = ((bf16[8,2,272,128]{3,2,1,0:T(8,128)(2,1)}), bf16[8,2,272,128]{3,2,1,0:T(8,128)(2,1)}, u32[]{:S(2)}, u32[]{:S(2)}) async-start(bf16[8,2,272,128]{3,2,1,0:T(8,128)(2,1)} %get-tuple-element.32.cot_ref), calls=%async_computation.2 | async-start | bytes 2228224 | tf_op jit(solution)/shard_map/all_to_all | solution.py:426
  207.3 1.4 reduce_sum.98
  209.6 28.5 %all-to-all-done.2.far_cot = bf16[8,2,272,128]{3,2,1,0:T(8,128)(2,1)} async-done(((bf16[8,2,272,128]{3,2,1,0:T(8,128)(2,1)}), bf16[8,2,272,128]{3,2,1,0:T(8,128)(2,1)}, u32[]{:S(2)}, u32[]{:S(2)}) %all-to-all-start.2) | async-done | bytes 1114144 | tf_op jit(solution)/shard_map/all_to_all | solution.py:426
  238.1 20.0 %near.1 = (bf16[2048,256]{1,0:T(8,128)(2,1)}, bf16[2048,256]{1,0:T(8,128)(2,1)}, bf16[2048,256]{1,0:T(8,128)(2,1)}, f32[2,256,256]{2,1,0:T(8,128)S(1)}) custom-call(s32[2,8]{1,0:T(2,128)S(1)} %and_select_fusion.4.slot, s32[2,8]{1,0:T(2,128)S(1)} %select_reduce_fusion.peer, s32[2]{0:T(128)S(1)} %get-tuple-element.45.c_idx.which.index, ...), custom_call_target="tpu_custom_call" | custom-call | flops 6710886400 | bytes 12582912 | tf_op jit(solution)/shard_map/near/pallas_call | solution.py:363
  259.8 1.3 slice.26
  261.7 2.2 patch.1
  (51 shorter events, 6.8 us)
Async XLA Ops:
  7.2 96.8 %all-gather.4.cloned.1.call-start = ((), (), s32[]{:S(2)}) async-start(), calls=%async_computation.4 | async-start | bytes 2359296 | tf_op jit(solution)/shard_map/all_gather | solution.py:463
  9.7 1.2 copy-start
  10.9 1.2 copy-start.2
  12.1 1.2 copy-start.4
  20.4 1.0 copy-start.10
  21.4 86.8 %copy-start.5 = (bf16[2048,256]{1,0:T(8,128)(2,1)S(1)}, bf16[2048,256]{1,0:T(8,128)(2,1)}, u32[]{:S(2)}) copy-start(bf16[2048,256]{1,0:T(8,128)(2,1)} %q_ref.7) | copy-start | bytes 3145732
  21.4 82.5 %all-to-all-start = ((bf16[8,2,256,256]{3,2,1,0:T(8,128)(2,1)}), bf16[8,2,256,256]{3,2,1,0:T(8,128)(2,1)}, u32[]{:S(2)}, u32[]{:S(2)}) async-start(bf16[8,2,256,256]{3,2,1,0:T(8,128)(2,1)} %get-tuple-element.25), calls=%async_computation | async-start | bytes 4194304 | tf_op jit(solution)/shard_map/all_to_all | solution.py:426
  28.9 79.3 %copy-start.1 = (bf16[2048,256]{1,0:T(8,128)(2,1)S(1)}, bf16[2048,256]{1,0:T(8,128)(2,1)}, u32[]{:S(2)}) copy-start(bf16[2048,256]{1,0:T(8,128)(2,1)} %k_ref.5) | copy-start | bytes 3145732
  28.9 79.4 %copy-start.3 = (bf16[2048,256]{1,0:T(8,128)(2,1)S(1)}, bf16[2048,256]{1,0:T(8,128)(2,1)}, u32[]{:S(2)}) copy-start(bf16[2048,256]{1,0:T(8,128)(2,1)} %v_ref.5) | copy-start | bytes 3145732
  28.9 79.3 %copy-start.14 = (f32[256]{0:T(256)S(1)}, f32[256]{0:T(256)}, u32[]{:S(2)}) copy-start(f32[256]{0:T(256)} %param.13) | copy-start | bytes 3076
  28.9 79.3 %copy-start.15 = (s32[2]{0:T(128)S(1)}, s32[2]{0:T(128)}, u32[]{:S(2)}) copy-start(s32[2]{0:T(128)} %count.3) | copy-start | bytes 28
  103.9 68.9 %all-to-all-start.1 = ((bf16[8,2,256,128]{3,2,1,0:T(8,128)(2,1)}), bf16[8,2,256,128]{3,2,1,0:T(8,128)(2,1)}, u32[]{:S(2)}, u32[]{:S(2)}) async-start(bf16[8,2,256,128]{3,2,1,0:T(8,128)(2,1)} %copy-done.10), calls=%async_computation.1 | async-start | bytes 2097152 | tf_op jit(solution)/shard_map/all_to_all | solution.py:426
  108.2 1.2 copy-start.6
  128.4 1.0 copy-start.8
  139.9 1.2 copy-start.7
  141.2 1.2 copy-start.9
  170.5 1.0 copy-start.11
  171.5 1.3 copy-start.16
  202.8 6.6 %copy-start.17 = (s32[2,64]{1,0:T(2,128)S(1)}, s32[2,64]{1,0:T(2,128)}, u32[]{:S(2)}) copy-start(s32[2,64]{1,0:T(2,128)} %param.11) | copy-start | bytes 1540
  202.8 35.2 %all-to-all-start.2 = ((bf16[8,2,272,128]{3,2,1,0:T(8,128)(2,1)}), bf16[8,2,272,128]{3,2,1,0:T(8,128)(2,1)}, u32[]{:S(2)}, u32[]{:S(2)}) async-start(bf16[8,2,272,128]{3,2,1,0:T(8,128)(2,1)} %get-tuple-element.32.cot_ref), calls=%async_computation.2 | async-start | bytes 2228224 | tf_op jit(solution)/shard_map/all_to_all | solution.py:426
  207.2 51.7 %all-gather.6.cloned.1.call-start = ((), (), s32[]{:S(2)}) async-start(), calls=%async_computation.5 | async-start | bytes 1253376 | tf_op jit(solution)/shard_map/all_gather | solution.py:490
  258.1 0.8 copy-start.12
  258.9 2.8 %copy-start.13 = (f32[2,256,256]{2,1,0:T(8,128)S(1)}, f32[2,256,256]{2,1,0:T(8,128)}, u32[]{:S(2)}) copy-start(f32[2,256,256]{2,1,0:T(8,128)} %copy-done.12) | copy-start | bytes 1572868
Sparse Core Ops, SparseCore 0:
  21.5 82.3 all-gather.3
  210.2 46.7 all-gather.5
